TPU v7x, 256 devices: a whole 4x4x8 slice. The times are simulated.
256 devices in a mesh: dp: 64 (over z, x, core), tensor: 4 (over y).
Axes of the slice: x: 4, y: 4, z: 8, core: 2. Of those that a mesh axis runs over, the one named last changes fastest.
Arguments:
- gradients: float32 [64, 128, 3, 28672], P('dp', None, None, 'tensor'), may hold values from -2097152 to 2097152
- token_counts: int32 [64, 3], P('dp'), may hold values from 512 to 6143
- modality: int32 [64], P('dp'), may hold values from 0 to 2
- loss_weight: float32 [3], replicated, may hold values from 0.5 to 2
- master: float32 [128, 3, 28672], P('dp', None, 'tensor'), may hold values from -6 to 6
- moment_one: float32 [128, 3, 28672], P('dp', None, 'tensor'), may hold values from -6 to 6
- moment_two: float32 [128, 3, 28672], P('dp', None, 'tensor'), may hold values from 0.05 to 2
Outputs:
- new_master: float32 [128, 3, 28672], P('dp', None, 'tensor')
- new_moment_one: float32 [128, 3, 28672], P('dp', None, 'tensor')
- new_moment_two: float32 [128, 3, 28672], P('dp', None, 'tensor')
- working_weights: bfloat16 [128, 3, 28672], P(None, None, 'tensor')
Inputs may be any that keep to these rules, and one draw needn't show every extreme that they name: `modality`: 0 is text, 1 image, 2 audio.
All inputs are finite; a program needn't handle non-finite values.
Results may differ from a plain program's by a relative error of at most 0.001.
Values may be sent and summed in bfloat16 or wider, within the bound.
No kernel may reach another device: no remote copies, remote signals or barrier semaphores. Data moves between devices by JAX's collectives and lax.ppermute only.
A program may use at most 128 MiB of HBM per device.

v0:
```python
import jax
import jax.numpy as jnp
from jax import lax
from jax.sharding import Mesh
from jax.sharding import PartitionSpec as P

DP = ("dp_0", "dp_1", "dp_2")


beta_one = 0.9
beta_two = 0.95
bias_one = 1.0 - 0.9**10
bias_two = 1.0 - 0.95**10
epsilon = 1e-08
learn_rate = 0.01
decay_rate = 0.1


def in_order(parts, dim):
    parts = jnp.moveaxis(parts, 0, dim)
    dims = parts.shape
    return parts.reshape(*dims[:dim], dims[dim] * dims[dim + 1], *dims[dim + 2 :])


def all_blocks(value, axes, turns):
    parts = value[None]
    for k in turns:
        parts = lax.all_gather(parts, axes[k], axis=0, tiled=True)
    current = [lax.axis_size(axes[k]) for k in reversed(turns)]
    parts = parts.reshape(*current, *value.shape)
    turned = sorted(range(len(turns)), key=lambda place: turns[len(turns) - 1 - place])
    return parts.transpose(*turned, *range(len(turns), parts.ndim)).reshape(-1, *value.shape)


def gather_axes(value, axes, turns, dim):
    return in_order(all_blocks(value, axes, turns), dim)


def from_everyone(value, axis):
    devices = lax.axis_size(axis)
    return lax.all_to_all(
        jnp.broadcast_to(value[None], (devices, *value.shape)), axis, 0, 0, tiled=True
    )


def taken_together(value, axis):
    return from_everyone(value, axis).sum(axis=0)


def scatter_axes(value, axes, dim):
    if not axes:
        return value
    nearer = lax.psum_scatter(value, axes[0], scatter_dimension=dim, tiled=True)
    return scatter_axes(nearer, axes[1:], dim)


def adam_update(grad_sum, first, second, weights):
    first_new = beta_one * first + (1.0 - beta_one) * grad_sum
    second_new = beta_two * second + (1.0 - beta_two) * grad_sum * grad_sum
    step_size = first_new / bias_one / (jnp.sqrt(second_new / bias_two) + epsilon)
    weights_new = weights - learn_rate * (step_size + decay_rate * weights)
    return (weights_new, first_new, second_new)


def publish(weights_new):
    return gather_axes(weights_new.astype(jnp.bfloat16), DP, (1, 0, 2), 0)


def local(gradients, token_counts, modality, loss_weight, master, moment_one, moment_two):
    totals = taken_together(token_counts[0], DP).astype(jnp.float32)
    ratios = loss_weight / totals
    picked = (lax.iota(jnp.int32, 3) == modality[0]).astype(jnp.float32)
    own_scale = jnp.sum(picked * ratios)
    replica_grad = gradients[0]
    summed = scatter_axes(replica_grad * own_scale, DP, 0)
    weights_new, first_new, second_new = adam_update(summed, moment_one, moment_two, master)
    return (weights_new, first_new, second_new, publish(weights_new))


def solution(mesh):
    torus = Mesh(
        mesh.devices.reshape(8, 4, 2, mesh.shape["tensor"]), ("dp_0", "dp_1", "dp_2", "tensor")
    )
    in_specs = (
        P(DP, None, None, "tensor"),
        P(DP, None),
        P(DP),
        P(),
        P(DP, None, "tensor"),
        P(DP, None, "tensor"),
        P(DP, None, "tensor"),
    )
    out_specs = (
        P(DP, None, "tensor"),
        P(DP, None, "tensor"),
        P(DP, None, "tensor"),
        P(None, None, "tensor"),
    )
    return jax.shard_map(local, mesh=torus, in_specs=in_specs, out_specs=out_specs, check_vma=False)
```

profile of v0, /device:TPU:1, one launch (start us, length us, event | category | flops | bytes accessed | tf_op | source)
XLA Modules:
  0.0 351.3 jit_solution(10869749909884527604)
XLA Ops:
  7.2 1.3 broadcast_in_dim.8
  8.5 13.0 %all-to-all-start = ((s32[64,1,3]{2,1,0:T(1,128)}), s32[64,1,3]{2,1,0:T(1,128)S(1)}, u32[]{:S(2)}, u32[]{:S(2)}) async-start(s32[64,1,3]{2,1,0:T(1,128)} %broadcast_in_dim.8), calls=%async_computation | async-start | bytes 65536 | tf_op jit(solution)/shard_map/all_to_all | solution.py:41
  21.4 0.0 reduce-scatter.4.cloned.1.call-start
  22.1 8.6 %all-to-all-done = s32[64,1,3]{2,1,0:T(1,128)S(1)} async-done(((s32[64,1,3]{2,1,0:T(1,128)}), s32[64,1,3]{2,1,0:T(1,128)S(1)}, u32[]{:S(2)}, u32[]{:S(2)}) %all-to-all-start) | async-done | bytes 800 | tf_op jit(solution)/shard_map/all_to_all | solution.py:41
  30.8 0.1 reduce_sum.18
  30.8 1.3 fusion.1
  32.1 10.2 %multiply_bitcast_fusion = f32[128,3,7168]{2,0,1:T(8,128)} fusion(f32[1,128,3,7168]{3,1,2,0:T(8,128)} %param.7, f32[]{:T(128)} %fusion.1), kind=kLoop, calls=%fused_computation | loop fusion | flops 2752512 | bytes 22020100 | tf_op jit(solution)/shard_map/mul | solution.py:75
  42.3 0.0 copy-start.4
  42.3 0.0 copy-start.3
  42.3 0.0 copy-start
  42.3 0.0 copy-start.1
  42.3 0.0 copy-start.2
  42.3 0.0 reduce-scatter.4.cloned.1.call-update
  42.4 0.0 all-reduce.5.cloned.1.call-start
  42.4 114.5 %reduce-scatter.4.cloned.1.call-done = f32[16,3,7168]{2,0,1:T(8,128)} async-done(((f32[128,3,7168]{2,0,1:T(8,128)}), f32[16,3,7168]{2,0,1:T(8,128)}) %reduce-scatter.4.cloned.1.call-update) | async-done | bytes 1376272 | tf_op jit(solution)/shard_map/reduce_scatter | solution.py:53
  156.9 0.0 all-reduce.5.cloned.1.call-update
  156.9 0.0 all-reduce.7.cloned.1.call-start
  157.0 0.0 copy-done.4
  157.0 0.6 dynamic-slice
  158.2 52.2 %all-reduce.5.cloned.1.call-done = f32[16,3,7168]{2,0,1:T(8,128)} async-done(((f32[16,3,7168]{2,0,1:T(8,128)}), f32[16,3,7168]{2,0,1:T(8,128)}) %all-reduce.5.cloned.1.call-update) | async-done | bytes 1376272
  210.4 1.9 constant_dynamic-slice_fusion
  212.3 0.0 all-reduce.7.cloned.1.call-update
  212.3 0.0 all-gather.4.cloned.1.call-start
  212.4 0.0 copy-done.3
  212.4 0.6 dynamic-slice.2
  213.6 31.2 %all-reduce.7.cloned.1.call-done = f32[4,3,7168]{2,0,1:T(4,128)} async-done(((f32[4,3,7168]{2,0,1:T(4,128)}), f32[4,3,7168]{2,0,1:T(4,128)}) %all-reduce.7.cloned.1.call-update) | async-done | bytes 344080
  244.8 0.0 copy-done
  244.8 0.0 copy-done.1
  244.8 0.0 copy-done.2
  244.8 2.4 fusion.2
  247.2 10.5 %all-gather = bf16[8,3,7168]{2,1,0:T(4,128)(2,1)S(1)} all-gather(bf16[2,3,7168]{2,1,0:T(4,128)(2,1)S(1)} %copy.25), channel_id=2, replica_groups=mesh['dp_0'=8,'dp_1'=4,'dp_2'=2,'tensor'=4] {'dp_1'}, dimensions={0}, use_global_device_ids=true | all-gather | bytes 430080 | tf_op jit(solution)/shard_map/all_gather | solution.py:28
  257.7 1.0 copy.26
  258.8 0.0 all-gather.4.cloned.1.call-update
  258.8 0.0 all-gather.6.cloned.1.call-start
  258.8 43.1 %all-gather.4.cloned.1.call-done = bf16[32,2,3,7168]{3,1,2,0:T(2,128)(2,1)} async-done(((bf16[4,2,3,7168]{3,1,2,0:T(2,128)(2,1)}), bf16[32,2,3,7168]{3,1,2,0:T(2,128)(2,1)}) %all-gather.4.cloned.1.call-update) | async-done | bytes 2752528 | tf_op jit(solution)/shard_map/all_gather | solution.py:28
  301.9 0.0 all-gather.6.cloned.1.call-update
  301.9 24.7 %all-gather.6.cloned.1.call-done = bf16[64,2,3,7168]{3,1,2,0:T(2,128)(2,1)} async-done(((bf16[32,2,3,7168]{3,1,2,0:T(2,128)(2,1)}), bf16[64,2,3,7168]{3,1,2,0:T(2,128)(2,1)}) %all-gather.6.cloned.1.call-update) | async-done | bytes 5505040 | tf_op jit(solution)/shard_map/all_gather | solution.py:28
  326.6 6.4 %copy.27 = bf16[8,4,2,2,3,7168]{5,3,2,1,0,4:T(2,128)(2,1)} copy(bf16[8,4,2,2,3,7168]{5,3,4,1,0,2:T(2,128)(2,1)} %bitcast.13) | data formatting | bytes 11010048 | tf_op jit(solution)/shard_map/transpose | solution.py:32
  333.0 11.8 %reshape_reshape.3 = bf16[128,3,7168]{2,0,1:T(8,128)(2,1)} reshape(bf16[8,4,2,2,3,7168]{5,3,2,1,0,4:T(2,128)(2,1)} %copy.27) | data formatting | bytes 11010048 | tf_op jit(solution)/shard_map/reshape;reshape | solution.py:22
  (1 shorter events, 0.0 us)
Async XLA Ops:
  8.5 22.3 %all-to-all-start = ((s32[64,1,3]{2,1,0:T(1,128)}), s32[64,1,3]{2,1,0:T(1,128)S(1)}, u32[]{:S(2)}, u32[]{:S(2)}) async-start(s32[64,1,3]{2,1,0:T(1,128)} %broadcast_in_dim.8), calls=%async_computation | async-start | bytes 65536 | tf_op jit(solution)/shard_map/all_to_all | solution.py:41
  21.4 135.5 %reduce-scatter.4.cloned.1.call-start = ((), (), s32[]{:S(2)}) async-start(), calls=%async_computation.2 | async-start | bytes 12386304 | tf_op jit(solution)/shard_map/reduce_scatter | solution.py:53
  42.3 114.7 %copy-start.4 = (u32[256]{0:T(256)S(1)}, u32[256]{0:T(256)}, u32[]{:S(2)}) copy-start(u32[256]{0:T(256)} %constant.31) | copy-start | bytes 3076
  42.3 170.0 %copy-start.3 = (u32[256]{0:T(256)S(1)}, u32[256]{0:T(256)}, u32[]{:S(2)}) copy-start(u32[256]{0:T(256)} %constant.35) | copy-start | bytes 3076
  42.3 202.4 %copy-start = (f32[2,3,7168]{2,0,1:T(2,128)S(1)}, f32[2,3,7168]{2,0,1:T(2,128)}, u32[]{:S(2)}) copy-start(f32[2,3,7168]{2,0,1:T(2,128)} %param.11) | copy-start | bytes 516100
  42.3 202.4 %copy-start.1 = (f32[2,3,7168]{2,0,1:T(2,128)S(1)}, f32[2,3,7168]{2,0,1:T(2,128)}, u32[]{:S(2)}) copy-start(f32[2,3,7168]{2,0,1:T(2,128)} %param.12) | copy-start | bytes 516100
  42.3 202.4 %copy-start.2 = (f32[2,3,7168]{2,0,1:T(2,128)S(1)}, f32[2,3,7168]{2,0,1:T(2,128)}, u32[]{:S(2)}) copy-start(f32[2,3,7168]{2,0,1:T(2,128)} %param.13) | copy-start | bytes 516100
  42.4 168.0 %all-reduce.5.cloned.1.call-start = ((), (), s32[]{:S(2)}) async-start(), calls=%async_computation.5 | async-start | bytes 2752512
  156.9 87.8 %all-reduce.7.cloned.1.call-start = ((), (), s32[]{:S(2)}) async-start(), calls=%async_computation.6 | async-start | bytes 688128
  212.3 89.6 %all-gather.4.cloned.1.call-start = ((), (), s32[]{:S(2)}) async-start(), calls=%async_computation.3 | async-start | bytes 3096576 | tf_op jit(solution)/shard_map/all_gather | solution.py:28
  258.8 67.8 %all-gather.6.cloned.1.call-start = ((), (), s32[]{:S(2)}) async-start(), calls=%async_computation.4 | async-start | bytes 8257536 | tf_op jit(solution)/shard_map/all_gather | solution.py:28
Sparse Core Ops, SparseCore 0:
  42.5 114.3 reduce-scatter.3
  159.3 51.0 all-reduce.4
  213.6 31.1 all-reduce.6
  258.9 42.9 all-gather.3
  303.6 23.0 all-gather.5
where the time goes:
time: 352 us; the launch traced here: 351 us
  waiting for transfers between devices  274 us (78%)
  local copies, waits for them, and re-layouts  23.7 us (7%)
  between operations  15.8 us (4%)
  other arithmetic  13.9 us (4%)
  starting transfers between devices  13.2 us (4%)
  blocking collectives  10.5 us (3%)
    reduce_scatter x1, waiting for transfers between devices, scatter_axes(): nearer = lax.psum_scatter(value, axes[0], scatter_dimension=dim, tiled=True)  114 us
    unnamed x7, waiting for transfers between devices  83.4 us
    all_gather x2, waiting for transfers between devices, all_blocks(): parts = lax.all_gather(parts, axes[k], axis=0, tiled=True)  67.7 us
    all_to_all x1, starting transfers between devices, from_everyone(): lax.all_to_all(jnp.broadcast_to(value[None], (devices, *value.shape)), ax...  13 us
    another operation x1, local copies, waits for them, and re-layouts, in_order(): parts.reshape(*dims[:dim], dims[dim] * dims[dim + 1], *dims[dim + 2:])  11.8 us
    all_gather x1, blocking collectives, all_blocks(): parts = lax.all_gather(parts, axes[k], axis=0, tiled=True)  10.5 us
    mul x1, other arithmetic, local(): summed = scatter_axes(replica_grad * own_scale, DP, 0)  10.2 us
    all_to_all x1, waiting for transfers between devices, from_everyone(): lax.all_to_all(jnp.broadcast_to(value[None], (devices, *value.shape)), ax...  8.63 us
  transfers between devices with their start and end apart: 6, of which 6 were waited for; matrix products, arithmetic and copies ran while one was open for 0% of the time, Pallas kernels for 0%

commit v1 on v0

v1 whole, which is shorter than its diff:
```python
import jax
import jax.numpy as jnp
from jax import lax
from jax.sharding import Mesh
from jax.sharding import PartitionSpec as P

DP = ("z", "x", "c")
DEEP, WIDE = 8, 4

beta_one = 0.9
beta_two = 0.95
bias_one = 1.0 - 0.9**10
bias_two = 1.0 - 0.95**10
epsilon = 1e-08
learn_rate = 0.01
decay_rate = 0.1

PART_A = 1536
RAISE = 4.0
LINK = jnp.float16


def adam_update(grad_sum, first, second, weights):
    first_new = beta_one * first + (1.0 - beta_one) * grad_sum
    second_new = beta_two * second + (1.0 - beta_two) * grad_sum * grad_sum
    step_size = first_new / bias_one / (jnp.sqrt(second_new / bias_two) + epsilon)
    weights_new = weights - learn_rate * (step_size + decay_rate * weights)
    return (weights_new, first_new, second_new)


def x_partner(step, z, x, c):
    return (z, x ^ (1 if step == c else 3), c)


def z_partner(step, z, x, c):
    if step == 2:
        return (z ^ 4, x, c)
    return ((((z + c) % DEEP) ^ (1 << step)) - c) % DEEP, x, c


def core_partner(step, z, x, c):
    return (z, x, 1 - c)


def trade(value, partner, step=0):
    def index(z, x, c):
        return (z * WIDE + x) * 2 + c

    perm = [
        (index(z, x, c), index(*partner(step, z, x, c)))
        for z in range(DEEP)
        for x in range(WIDE)
        for c in range(2)
    ]
    return lax.ppermute(value, DP, perm)


def x_bits(x, c):
    high, mixed = x // 2, (x + x // 2) % 2
    return (mixed * (1 - c) + high * c, high * (1 - c) + mixed * c)


def pick(value, index, parts, dim):
    size = value.shape[dim] // parts
    return lax.dynamic_slice_in_dim(value, index * size, size, dim)


def sum_x(value, bits):
    for step in range(2):
        got = trade(pick(value, 1 - bits[step], 2, 2).astype(LINK), x_partner, step)
        value = pick(value, bits[step], 2, 2) + got.astype(jnp.float32)
    return value


def pick_rows(value, index):
    mats, rows, cols = value.shape
    split = value.reshape(mats, rows // 32, 2, 16, cols)
    return lax.dynamic_slice_in_dim(split, index, 1, 2).reshape(mats, rows // 2, cols)


def sum_z(value, depth):
    for step in range(3):
        bit = (depth // 2**step) % 2
        got = trade(pick_rows(value, 1 - bit).astype(LINK), z_partner, step)
        value = pick_rows(value, bit) + got.astype(jnp.float32)
    return value


def both(own, got, bit, dim):
    first = jnp.where(bit == 0, own, got)
    second = jnp.where(bit == 0, got, own)
    return jnp.concatenate([first, second], axis=dim)


def gather_x(value, bits):
    for step in (1, 0):
        value = both(value, trade(value, x_partner, step), bits[step], 2)
    return value


def gather_z(value, depth):
    mats, _, cols = value.shape
    for step in (2, 1, 0):
        got = trade(value, z_partner, step)
        bit = (depth // 2**step) % 2
        rows = value.shape[1]
        own, got = (v.reshape(mats, rows // 16, 1, 16, cols) for v in (value, got))
        value = both(own, got, bit, 2).reshape(mats, 2 * rows, cols)
    return value


def split_columns(state, wide_a, across, mine, bits):
    keep = pick(state, mine, 2, 3)
    got = trade(pick(state, 1 - mine, 2, 3), core_partner)
    rows = both(keep, got, mine, 2)
    groups = [(rows[..., :wide_a], rows[..., wide_a:])]
    for step in range(2):
        give = [[pick(v, 1 - bits[step], 2, 3) for v in group] for group in groups]
        flat = jnp.concatenate([jnp.concatenate(g, axis=3) for g in give], axis=2)
        got = trade(flat, x_partner, step)
        cut = give[0][0].shape[3]
        groups = [tuple(pick(v, bits[step], 2, 3) for v in group) for group in groups]
        for k in range(len(give)):
            piece = got[:, :, 4 * k : 4 * k + 4]
            groups.append((piece[..., :cut], piece[..., cut:]))
    masks = (1 + 2 * mine, 3 - 2 * mine)
    places = (across, across ^ masks[0], across ^ masks[1], across ^ masks[0] ^ masks[1])
    whole = jnp.zeros((*state.shape[:2], 16, state.shape[3] // 8), state.dtype)
    for place, group in zip(places, groups):
        whole = lax.dynamic_update_slice_in_dim(whole, jnp.concatenate(group, axis=3), 4 * place, 2)
    return whole


def join_columns(state, wide_a, across, mine, bits):
    masks = (1 + 2 * mine, 3 - 2 * mine)
    places = (across, across ^ masks[0], across ^ masks[1], across ^ masks[0] ^ masks[1])
    own, one, two, three = [pick(state, place, 4, 2) for place in places]
    got = trade(jnp.concatenate([one, three], axis=2), x_partner, 0)
    mine_now = [own, got[:, :, :4]]
    got = trade(jnp.concatenate([two, got[:, :, 4:]], axis=2), x_partner, 1)
    chunks = [*mine_now, got[:, :, :4], got[:, :, 4:]]
    place = 2 * bits[0] + bits[1]
    cut, rest = wide_a // 4, state.shape[3] - wide_a // 4
    left = jnp.zeros((*state.shape[:2], 4, 4 * state.shape[3]), state.dtype)
    for chunk, flip in zip(chunks, (0, 2, 1, 3)):
        at = place ^ flip
        left = lax.dynamic_update_slice_in_dim(left, chunk[..., :cut], cut * at, 3)
        left = lax.dynamic_update_slice_in_dim(left, chunk[..., cut:], wide_a + rest * at, 3)
    keep = pick(left, mine, 2, 2)
    got = trade(pick(left, 1 - mine, 2, 2), core_partner)
    return both(keep, got, mine, 3)


def local(gradients, token_counts, modality, loss_weight, master, moment_one, moment_two):
    grad = jnp.transpose(gradients[0], (1, 0, 2))
    mats, rows, cols = grad.shape
    half = cols // 2
    wide_a, wide_b = PART_A, half - PART_A
    depth, across, mine = (lax.axis_index(a) for a in DP)
    bits = x_bits(across, mine)

    counts = jnp.broadcast_to(token_counts, (DEEP * WIDE * 2, 3))[:, None]
    totals = lax.all_to_all(counts, DP, 0, 0, tiled=True).sum(axis=(0, 1)).astype(jnp.float32)

    here, there = mine * half, (1 - mine) * half
    raw_a = trade(lax.dynamic_slice_in_dim(grad, there, wide_a, 2), core_partner)
    raw_b = trade(lax.dynamic_slice_in_dim(grad, there + wide_a, wide_b, 2), core_partner)

    ratios = loss_weight / totals
    kinds = jnp.concatenate([modality, trade(modality, core_partner)])
    picked = (lax.iota(jnp.int32, 3)[None, :] == kinds[:, None]).astype(jnp.float32)
    scales = jnp.sum(picked * ratios[None, :], axis=1) * RAISE

    own_a = lax.dynamic_slice_in_dim(grad, here, wide_a, 2)
    own_b = lax.dynamic_slice_in_dim(grad, here + wide_a, wide_b, 2)
    sum_a = sum_x(sum_z(own_a * scales[0] + raw_a * scales[1], depth), bits)
    sum_b = sum_z(sum_x(own_b * scales[0] + raw_b * scales[1], bits), depth)
    summed = jnp.concatenate([sum_a, sum_b], axis=2) * (1.0 / RAISE)

    state = jnp.stack([jnp.transpose(a, (1, 0, 2)) for a in (master, moment_one, moment_two)])
    state = split_columns(state, wide_a, across, mine, bits)
    new = adam_update(summed, state[1], state[2], state[0])
    lean = new[0].astype(jnp.bfloat16)

    lean_a = gather_z(gather_x(lean[..., : wide_a // 4], bits), depth)
    lean_b = gather_x(gather_z(lean[..., wide_a // 4 :], depth), bits)
    far_a, far_b = trade(lean_a, core_partner), trade(lean_b, core_partner)
    whole = jnp.zeros((mats, rows, cols), jnp.bfloat16)
    for at, piece in ((here, lean_a), (here + wide_a, lean_b), (there, far_a), (there + wide_a, far_b)):
        whole = lax.dynamic_update_slice_in_dim(whole, piece, at, 2)

    back = join_columns(jnp.stack(new), wide_a, across, mine, bits)
    outs = [jnp.transpose(back[i], (1, 0, 2)) for i in range(3)]
    return (*outs, jnp.transpose(whole, (1, 0, 2)))


def solution(mesh):
    torus = Mesh(mesh.devices.reshape(DEEP, WIDE, 2, mesh.shape["tensor"]), (*DP, "tensor"))
    in_specs = (
        P(DP, None, None, "tensor"),
        P(DP, None),
        P(DP),
        P(),
        P(DP, None, "tensor"),
        P(DP, None, "tensor"),
        P(DP, None, "tensor"),
    )
    out_specs = (
        P(DP, None, "tensor"),
        P(DP, None, "tensor"),
        P(DP, None, "tensor"),
        P(None, None, "tensor"),
    )
    return jax.shard_map(local, mesh=torus, in_specs=in_specs, out_specs=out_specs, check_vma=False)
```

time: 352 us -> 161 us (0.46)
  waiting for transfers between devices: 274 us -> 44.5 us
  starting transfers between devices: 13.2 us -> 85 us
  between operations: 15.8 us -> 2.03 us
  local copies, waits for them, and re-layouts: 23.7 us -> 12.2 us
  blocking collectives: 10.5 us -> 0 us
    reduce_scatter x1 -> x0, waiting for transfers between devices: 114 us -> none  [scatter_axes(): nearer = lax.psum_scatter(value, axes[0], scatter_dimension=dim, tiled=True)]
    unnamed x7 -> x0, waiting for transfers between devices: 83.4 us -> none
    ppermute x0 -> x31, starting transfers between devices: none -> 75.1 us  [trade(): return lax.ppermute(value, DP, perm)]
    all_gather x2 -> x0, waiting for transfers between devices: 67.7 us -> none  [all_blocks(): parts = lax.all_gather(parts, axes[k], axis=0, tiled=True)]
    ppermute x0 -> x31, waiting for transfers between devices: none -> 44.5 us  [trade(): return lax.ppermute(value, DP, perm)]
    another operation x1, local copies, waits for them, and re-layouts: 11.8 us -> 1.29 us  [local(): counts = jnp.broadcast_to(token_counts, (DEEP * WIDE * 2, 3))[:, None]]
    all_gather x1 -> x0, blocking collectives: 10.5 us -> none  [all_blocks(): parts = lax.all_gather(parts, axes[k], axis=0, tiled=True)]
    mul x1, other arithmetic: 10.2 us -> 0.01 us  [local(): scales = jnp.sum(picked * ratios[None, :], axis=1) * RAISE]
  transfers between devices with their start and end apart: 6 -> 32, of which waited for: 6 -> 16; matrix products, arithmetic and copies ran while one was open for 0% -> 16% of each run, Pallas kernels for 0% -> 0%
where the time goes in v1:
time: 161 us
  starting transfers between devices  85 us (53%)
  waiting for transfers between devices  44.5 us (28%)
  other arithmetic  17.1 us (11%)
  local copies, waits for them, and re-layouts  12.2 us (8%)
  between operations  2.03 us (1%)
    ppermute x31, starting transfers between devices, trade(): return lax.ppermute(value, DP, perm)  75.1 us
    ppermute x31, waiting for transfers between devices, trade(): return lax.ppermute(value, DP, perm)  44.5 us
    all_to_all x1, starting transfers between devices, local(): lax.all_to_all(counts, DP, 0, 0, tiled=True).sum(axis=(0, 1))  9.89 us
    add x1, other arithmetic, local(): sum_b = sum_z(sum_x(own_b * scales[0] + raw_b * scales[1], bits), depth)  5.03 us
    add x1, other arithmetic, local(): sum_a = sum_x(sum_z(own_a * scales[0] + raw_a * scales[1], depth), bits)  4.13 us
    dynamic_slice x1, local copies, waits for them, and re-layouts, local(): lax.dynamic_slice_in_dim(grad, there + wide_a, wide_b, 2)  3.92 us
  transfers between devices with their start and end apart: 32, of which 16 were waited for; matrix products, arithmetic and copies ran while one was open for 16% of the time, Pallas kernels for 0%

profile of v1, /device:TPU:1, one launch (start us, length us, event | category | flops | bytes accessed | tf_op | source)
XLA Modules:
  0.0 160.8 jit_solution(4804430294184326411)
XLA Ops:
  0.6 3.3 %collective-permute-start.3 = (s32[1]{0:T(128)}, s32[1]{0:T(128)}, u32[]{:S(2)}, u32[]{:S(2)}) collective-permute-start(s32[1]{0:T(128)} %param.9), channel_id=1, source_target_pairs={{0,4},{4,0},{8,12},{12,8},{16,20},{20,16},{24,28},{28,24},{32,36},... | collective-permute-start | bytes 20 | tf_op jit(solution)/shard_map/ppermute | solution.py:55
  3.9 1.3 broadcast_in_dim_broadcast_in_dim.2
  5.2 9.9 %all-to-all-start = ((s32[64,1,3]{2,1,0:T(1,128)}), s32[64,1,3]{2,1,0:T(1,128)S(1)}, u32[]{:S(2)}, u32[]{:S(2)}) async-start(s32[64,1,3]{2,1,0:T(1,128)} %broadcast_in_dim_broadcast_in_dim.2), calls=%async_computation | async-start | bytes 65536 | tf_op jit(solution)/shard_map/all_to_all | solution.py:163
  15.1 1.3 pad_maximum_fusion.4
  16.5 0.5 collective-permute-start
  17.0 1.8 %dynamic-slice_bitcast_fusion.1 = f32[3,128,1536]{2,1,0:T(8,128)S(1)} fusion(f32[1,128,3,7168]{3,1,2,0:T(8,128)} %param.7, s32[]{:T(128)S(6)} %select_n.412), kind=kLoop, calls=%fused_computation.3 | loop fusion | bytes 4718596 | tf_op jit(solution)/shard_map/dynamic_slice | solution.py:166
  19.0 3.9 %dynamic-slice_bitcast_fusion = f32[3,128,2048]{2,1,0:T(8,128)} fusion(f32[1,128,3,7168]{3,1,2,0:T(8,128)} %param.7, s32[]{:T(128)S(6)} %select_n.447), kind=kLoop, calls=%fused_computation.1 | loop fusion | bytes 6291460 | tf_op jit(solution)/shard_map/dynamic_slice | solution.py:167
  24.0 0.7 pad_add_fusion
  25.6 2.6 %collective-permute-start.1 = (f32[3,3,4,1792]{3,2,1,0:T(4,128)S(1)}, f32[3,3,4,1792]{3,2,1,0:T(4,128)S(1)}, u32[]{:S(2)}, u32[]{:S(2)}) collective-permute-start(f32[3,3,4,1792]{3,2,1,0:T(4,128)S(1)} %pad_maximum_fusion.8), channel_id=1, source_target_pairs={{0,8},{4,28},{8,0},{12,20},{16,24},{20,12},{24,16},{28,4},{32,40},... | collective-permute-start | bytes 774152 | tf_op jit(solution)/shard_map/ppermute | solution.py:55
  28.2 0.6 fusion.23
  29.2 2.9 %collective-permute-done.1 = f32[3,3,4,1792]{3,2,1,0:T(4,128)S(1)} collective-permute-done((f32[3,3,4,1792]{3,2,1,0:T(4,128)S(1)}, f32[3,3,4,1792]{3,2,1,0:T(4,128)S(1)}, u32[]{:S(2)}, u32[]{:S(2)}) %collective-permute-start.1) | collective-permute-done | bytes 258080 | tf_op jit(solution)/shard_map/ppermute | solution.py:55
  32.2 4.1 %bitcast_add_fusion.1 = f32[3,128,1536]{2,1,0:T(8,128)S(1)} fusion(f32[3,128,1536]{2,1,0:T(8,128)} %collective-permute-done.4, f32[1,128,3,7168]{3,1,2,0:T(8,128)} %param.7, s32[]{:T(128)S(6)} %select_n.411, f32[]{:T(128)} %bitcast.12, f32[]{:T(128)} %bitcast.7), kind=kLoop, calls=%fused_computation.2 | loop fusion | flops 1769472 | bytes 7077900 | tf_op jit(solution)/shard_map/add | solution.py:176
  36.5 2.9 %collective-permute-start.5 = (f16[3,64,1536]{2,1,0:T(8,128)(2,1)S(1)}, f16[3,64,1536]{2,1,0:T(8,128)(2,1)S(1)}, u32[]{:S(2)}, u32[]{:S(2)}) collective-permute-start(f16[3,64,1536]{2,1,0:T(8,128)(2,1)S(1)} %bitcast.156), channel_id=1, source_target_pairs={{0,32},{4,228},{8,40},{12,236},{16,48},{20,244},{24,56},{28,252},{... | collective-permute-start | bytes 1769480 | tf_op jit(solution)/shard_map/ppermute | solution.py:55
  40.0 5.0 %collective-permute-done.2 = f32[3,3,8,896]{3,2,1,0:T(8,128)S(1)} collective-permute-done((f32[3,3,8,896]{3,2,1,0:T(8,128)S(1)}, f32[3,3,8,896]{3,2,1,0:T(8,128)S(1)}, u32[]{:S(2)}, u32[]{:S(2)}) %collective-permute-start.2) | collective-permute-done | bytes 258080 | tf_op jit(solution)/shard_map/ppermute | solution.py:55
  45.0 1.6 collective-permute-done.5
  46.9 1.3 collective-permute-start.6
  48.2 5.0 %bitcast_add_fusion = f32[3,128,2048]{2,1,0:T(8,128)S(1)} fusion(f32[3,128,2048]{2,1,0:T(8,128)} %collective-permute-done.10, f32[1,128,3,7168]{3,1,2,0:T(8,128)} %param.7, s32[]{:T(128)S(6)} %select_n.446, f32[]{:T(128)} %bitcast.12, f32[]{:T(128)} %bitcast.7), kind=kLoop, calls=%fused_computation | loop fusion | flops 2359296 | bytes 9437196 | tf_op jit(solution)/shard_map/add | solution.py:177
  53.4 2.5 %collective-permute-start.11 = (f16[3,128,1024]{2,1,0:T(8,128)(2,1)S(1)}, f16[3,128,1024]{2,1,0:T(8,128)(2,1)S(1)}, u32[]{:S(2)}, u32[]{:S(2)}) collective-permute-start(f16[3,128,1024]{2,1,0:T(8,128)(2,1)S(1)} %dynamic-slice_convert_fusion), channel_id=1, source_target_pairs={{0,8},{4,28},{8,0},{12,20},{16,24},{20,12},{24,16},{28,4},{32,40},... | collective-permute-start | bytes 2359304 | tf_op jit(solution)/shard_map/ppermute | solution.py:55
  55.9 3.6 %collective-permute-done.6 = f16[3,32,1536]{2,1,0:T(8,128)(2,1)S(1)} collective-permute-done((f16[3,32,1536]{2,1,0:T(8,128)(2,1)S(1)}, f16[3,32,1536]{2,1,0:T(8,128)(2,1)S(1)}, u32[]{:S(2)}, u32[]{:S(2)}) %collective-permute-start.6) | collective-permute-done | bytes 294944 | tf_op jit(solution)/shard_map/ppermute | solution.py:55
  59.6 5.4 %collective-permute-start.7 = (f16[3,16,1536]{2,1,0:T(8,128)(2,1)S(1)}, f16[3,16,1536]{2,1,0:T(8,128)(2,1)S(1)}, u32[]{:S(2)}, u32[]{:S(2)}) collective-permute-start(f16[3,16,1536]{2,1,0:T(8,128)(2,1)S(1)} %fusion.15), channel_id=1, source_target_pairs={{0,128},{4,132},{8,136},{12,140},{16,144},{20,148},{24,152},{28,15... | collective-permute-start | bytes 442376 | tf_op jit(solution)/shard_map/ppermute | solution.py:55
  65.0 0.5 collective-permute-done.11
  65.9 2.0 %collective-permute-done.7 = f16[3,16,1536]{2,1,0:T(8,128)(2,1)S(1)} collective-permute-done((f16[3,16,1536]{2,1,0:T(8,128)(2,1)S(1)}, f16[3,16,1536]{2,1,0:T(8,128)(2,1)S(1)}, u32[]{:S(2)}, u32[]{:S(2)}) %collective-permute-start.7) | collective-permute-done | bytes 147488 | tf_op jit(solution)/shard_map/ppermute | solution.py:55
  68.0 2.6 %collective-permute-start.8 = (f16[3,16,768]{2,1,0:T(8,128)(2,1)S(1)}, f16[3,16,768]{2,1,0:T(8,128)(2,1)S(1)}, u32[]{:S(2)}, u32[]{:S(2)}) collective-permute-start(f16[3,16,768]{2,1,0:T(8,128)(2,1)S(1)} %dynamic-slice_convert_fusion.5), channel_id=1, source_target_pairs={{0,8},{4,28},{8,0},{12,20},{16,24},{20,12},{24,16},{28,4},{32,40},... | collective-permute-start | bytes 221192 | tf_op jit(solution)/shard_map/ppermute | solution.py:55
  70.6 2.0 %collective-permute-done.12 = f16[3,128,512]{2,1,0:T(8,128)(2,1)S(1)} collective-permute-done((f16[3,128,512]{2,1,0:T(8,128)(2,1)S(1)}, f16[3,128,512]{2,1,0:T(8,128)(2,1)S(1)}, u32[]{:S(2)}, u32[]{:S(2)}) %collective-permute-start.12) | collective-permute-done | bytes 393248 | tf_op jit(solution)/shard_map/ppermute | solution.py:55
  72.8 2.2 %collective-permute-start.13 = (f16[3,64,512]{2,1,0:T(8,128)(2,1)S(1)}, f16[3,64,512]{2,1,0:T(8,128)(2,1)S(1)}, u32[]{:S(2)}, u32[]{:S(2)}) collective-permute-start(f16[3,64,512]{2,1,0:T(8,128)(2,1)S(1)} %bitcast.161), channel_id=1, source_target_pairs={{0,32},{4,228},{8,40},{12,236},{16,48},{20,244},{24,56},{28,252},{... | collective-permute-start | bytes 589832 | tf_op jit(solution)/shard_map/ppermute | solution.py:55
  75.0 3.6 %collective-permute-done.13 = f16[3,64,512]{2,1,0:T(8,128)(2,1)S(1)} collective-permute-done((f16[3,64,512]{2,1,0:T(8,128)(2,1)S(1)}, f16[3,64,512]{2,1,0:T(8,128)(2,1)S(1)}, u32[]{:S(2)}, u32[]{:S(2)}) %collective-permute-start.13) | collective-permute-done | bytes 196640 | tf_op jit(solution)/shard_map/ppermute | solution.py:55
  78.7 2.9 %collective-permute-start.14 = (f16[3,32,512]{2,1,0:T(8,128)(2,1)S(1)}, f16[3,32,512]{2,1,0:T(8,128)(2,1)S(1)}, u32[]{:S(2)}, u32[]{:S(2)}) collective-permute-start(f16[3,32,512]{2,1,0:T(8,128)(2,1)S(1)} %bitcast.168), channel_id=1, source_target_pairs={{0,64},{4,68},{8,72},{12,76},{16,80},{20,84},{24,88},{28,92},{32,9... | collective-permute-start | bytes 294920 | tf_op jit(solution)/shard_map/ppermute | solution.py:55
  81.7 2.0 %collective-permute-done.14 = f16[3,32,512]{2,1,0:T(8,128)(2,1)S(1)} collective-permute-done((f16[3,32,512]{2,1,0:T(8,128)(2,1)S(1)}, f16[3,32,512]{2,1,0:T(8,128)(2,1)S(1)}, u32[]{:S(2)}, u32[]{:S(2)}) %collective-permute-start.14) | collective-permute-done | bytes 98336 | tf_op jit(solution)/shard_map/ppermute | solution.py:55
  83.8 3.9 %collective-permute-start.15 = (f16[3,16,512]{2,1,0:T(8,128)(2,1)S(1)}, f16[3,16,512]{2,1,0:T(8,128)(2,1)S(1)}, u32[]{:S(2)}, u32[]{:S(2)}) collective-permute-start(f16[3,16,512]{2,1,0:T(8,128)(2,1)S(1)} %fusion.21), channel_id=1, source_target_pairs={{0,128},{4,132},{8,136},{12,140},{16,144},{20,148},{24,152},{28,15... | collective-permute-start | bytes 147464 | tf_op jit(solution)/shard_map/ppermute | solution.py:55
  87.7 3.6 %collective-permute-done.15 = f16[3,16,512]{2,1,0:T(8,128)(2,1)S(1)} collective-permute-done((f16[3,16,512]{2,1,0:T(8,128)(2,1)S(1)}, f16[3,16,512]{2,1,0:T(8,128)(2,1)S(1)}, u32[]{:S(2)}, u32[]{:S(2)}) %collective-permute-start.15) | collective-permute-done | bytes 49184 | tf_op jit(solution)/shard_map/ppermute | solution.py:55
  91.9 3.4 %collective-permute-start.24 = (bf16[3,16,512]{2,1,0:T(8,128)(2,1)S(1)}, bf16[3,16,512]{2,1,0:T(8,128)(2,1)S(1)}, u32[]{:S(2)}, u32[]{:S(2)}) collective-permute-start(bf16[3,16,512]{2,1,0:T(8,128)(2,1)S(1)} %slice.132), channel_id=1, source_target_pairs={{0,128},{4,132},{8,136},{12,140},{16,144},{20,148},{24,152},{28,15... | collective-permute-start | bytes 147464 | tf_op jit(solution)/shard_map/ppermute | solution.py:55
  95.3 2.5 %collective-permute-start.16 = (f32[3,3,8,896]{3,2,1,0:T(8,128)S(1)}, f32[3,3,8,896]{3,2,1,0:T(8,128)S(1)}, u32[]{:S(2)}, u32[]{:S(2)}) collective-permute-start(f32[3,3,8,896]{3,2,1,0:T(8,128)S(1)} %pad_maximum_fusion.9), channel_id=1, source_target_pairs={{0,8},{4,28},{8,0},{12,20},{16,24},{20,12},{24,16},{28,4},{32,40},... | collective-permute-start | bytes 774152 | tf_op jit(solution)/shard_map/ppermute | solution.py:55
  98.4 0.7 collective-permute-done.24
  99.1 2.6 %collective-permute-start.25 = (bf16[3,32,512]{2,1,0:T(8,128)(2,1)S(1)}, bf16[3,32,512]{2,1,0:T(8,128)(2,1)S(1)}, u32[]{:S(2)}, u32[]{:S(2)}) collective-permute-start(bf16[3,32,512]{2,1,0:T(8,128)(2,1)S(1)} %bitcast.166), channel_id=1, source_target_pairs={{0,64},{4,68},{8,72},{12,76},{16,80},{20,84},{24,88},{28,92},{32,9... | collective-permute-start | bytes 294920 | tf_op jit(solution)/shard_map/ppermute | solution.py:55
  101.7 0.8 collective-permute-done.20
  102.6 2.2 %collective-permute-start.21 = (bf16[3,16,1536]{2,1,0:T(8,128)(2,1)S(1)}, bf16[3,16,1536]{2,1,0:T(8,128)(2,1)S(1)}, u32[]{:S(2)}, u32[]{:S(2)}) collective-permute-start(bf16[3,16,1536]{2,1,0:T(8,128)(2,1)S(1)} %pad_maximum_fusion.15), channel_id=1, source_target_pairs={{0,128},{4,132},{8,136},{12,140},{16,144},{20,148},{24,152},{28,15... | collective-permute-start | bytes 442376 | tf_op jit(solution)/shard_map/ppermute | solution.py:55
  104.9 4.1 %collective-permute-start.26 = (bf16[3,64,512]{2,1,0:T(8,128)(2,1)S(1)}, bf16[3,64,512]{2,1,0:T(8,128)(2,1)S(1)}, u32[]{:S(2)}, u32[]{:S(2)}) collective-permute-start(bf16[3,64,512]{2,1,0:T(8,128)(2,1)S(1)} %bitcast.151), channel_id=1, source_target_pairs={{0,32},{4,228},{8,40},{12,236},{16,48},{20,244},{24,56},{28,252},{... | collective-permute-start | bytes 589832 | tf_op jit(solution)/shard_map/ppermute | solution.py:55
  109.1 1.1 collective-permute-start.17
  110.1 4.2 %collective-permute-done.21 = bf16[3,16,1536]{2,1,0:T(8,128)(2,1)S(1)} collective-permute-done((bf16[3,16,1536]{2,1,0:T(8,128)(2,1)S(1)}, bf16[3,16,1536]{2,1,0:T(8,128)(2,1)S(1)}, u32[]{:S(2)}, u32[]{:S(2)}) %collective-permute-start.21) | collective-permute-done | bytes 147488 | tf_op jit(solution)/shard_map/ppermute | solution.py:55
  115.0 8.6 %collective-permute-done.22 = bf16[3,32,1536]{2,1,0:T(8,128)(2,1)S(1)} collective-permute-done((bf16[3,32,1536]{2,1,0:T(8,128)(2,1)S(1)}, bf16[3,32,1536]{2,1,0:T(8,128)(2,1)S(1)}, u32[]{:S(2)}, u32[]{:S(2)}) %collective-permute-start.22) | collective-permute-done | bytes 294944 | tf_op jit(solution)/shard_map/ppermute | solution.py:55
  123.7 7.7 %collective-permute-start.23 = (bf16[3,64,1536]{2,1,0:T(8,128)(2,1)S(1)}, bf16[3,64,1536]{2,1,0:T(8,128)(2,1)S(1)}, u32[]{:S(2)}, u32[]{:S(2)}) collective-permute-start(bf16[3,64,1536]{2,1,0:T(8,128)(2,1)S(1)} %bitcast.144), channel_id=1, source_target_pairs={{0,32},{4,228},{8,40},{12,236},{16,48},{20,244},{24,56},{28,252},{... | collective-permute-start | bytes 1769480 | tf_op jit(solution)/shard_map/ppermute | solution.py:55
  131.6 10.1 %collective-permute-start.18 = (f32[3,3,2,3584]{3,2,1,0:T(2,128)S(1)}, f32[3,3,2,3584]{3,2,1,0:T(2,128)S(1)}, u32[]{:S(2)}, u32[]{:S(2)}) collective-permute-start(f32[3,3,2,3584]{3,2,1,0:T(2,128)S(1)} %constant_dynamic-slice_fusion), channel_id=1, source_target_pairs={{0,4},{4,0},{8,12},{12,8},{16,20},{20,16},{24,28},{28,24},{32,36},... | collective-permute-start | bytes 774152 | tf_op jit(solution)/shard_map/ppermute | solution.py:55
  142.4 9.4 %collective-permute-start.29 = (bf16[3,128,1536]{2,1,0:T(8,128)(2,1)S(1)}, bf16[3,128,1536]{2,1,0:T(8,128)(2,1)S(1)}, u32[]{:S(2)}, u32[]{:S(2)}) collective-permute-start(bf16[3,128,1536]{2,1,0:T(8,128)(2,1)S(1)} %bitcast.140), channel_id=1, source_target_pairs={{0,4},{4,0},{8,12},{12,8},{16,20},{20,16},{24,28},{28,24},{32,36},... | collective-permute-start | bytes 3538952 | tf_op jit(solution)/shard_map/ppermute | solution.py:55
  151.8 0.6 broadcast_in_dim.14
  152.6 1.4 collective-permute-done.28
  155.0 0.9 fusion.2
  156.1 2.1 %collective-permute-done.30 = bf16[3,128,2048]{2,1,0:T(8,128)(2,1)S(1)} collective-permute-done((bf16[3,128,2048]{2,1,0:T(8,128)(2,1)S(1)}, bf16[3,128,2048]{2,1,0:T(8,128)(2,1)S(1)}, u32[]{:S(2)}, u32[]{:S(2)}) %collective-permute-start.30) | collective-permute-done | bytes 1572896 | tf_op jit(solution)/shard_map/ppermute | solution.py:55
  158.4 2.4 %copy-done = bf16[3,128,7168]{2,1,0:T(8,128)(2,1)} copy-done((bf16[3,128,7168]{2,1,0:T(8,128)(2,1)}, bf16[3,128,7168]{2,1,0:T(8,128)(2,1)S(1)}, u32[]{:S(2)}) %copy-start) | copy-done | bytes 5505048
  (120 shorter events, 8.5 us)
Async XLA Ops:
  0.6 23.4 %collective-permute-start.3 = (s32[1]{0:T(128)}, s32[1]{0:T(128)}, u32[]{:S(2)}, u32[]{:S(2)}) collective-permute-start(s32[1]{0:T(128)} %param.9), channel_id=1, source_target_pairs={{0,4},{4,0},{8,12},{12,8},{16,20},{20,16},{24,28},{28,24},{32,36},... | collective-permute-start | bytes 20 | tf_op jit(solution)/shard_map/ppermute | solution.py:55
  5.2 19.6 %all-to-all-start = ((s32[64,1,3]{2,1,0:T(1,128)}), s32[64,1,3]{2,1,0:T(1,128)S(1)}, u32[]{:S(2)}, u32[]{:S(2)}) async-start(s32[64,1,3]{2,1,0:T(1,128)} %broadcast_in_dim_broadcast_in_dim.2), calls=%async_computation | async-start | bytes 65536 | tf_op jit(solution)/shard_map/all_to_all | solution.py:163
  16.5 8.6 %collective-permute-start = (f32[3,3,2,3584]{3,2,1,0:T(2,128)S(1)}, f32[3,3,2,3584]{3,2,1,0:T(2,128)S(1)}, u32[]{:S(2)}, u32[]{:S(2)}) collective-permute-start(f32[3,3,2,3584]{3,2,1,0:T(2,128)S(1)} %constant_dynamic-slice_fusion.12), channel_id=1, source_target_pairs={{0,4},{4,0},{8,12},{12,8},{16,20},{20,16},{24,28},{28,24},{32,36},... | collective-permute-start | bytes 774152 | tf_op jit(solution)/shard_map/ppermute | solution.py:55
  18.8 13.4 %collective-permute-start.4 = (f32[3,128,1536]{2,1,0:T(8,128)S(1)}, f32[3,128,1536]{2,1,0:T(8,128)}, u32[]{:S(2)}, u32[]{:S(2)}) collective-permute-start(f32[3,128,1536]{2,1,0:T(8,128)S(1)} %dynamic-slice_bitcast_fusion.1), channel_id=1, source_target_pairs={{0,4},{4,0},{8,12},{12,8},{16,20},{20,16},{24,28},{28,24},{32,36},... | collective-permute-start | bytes 7077896 | tf_op jit(solution)/shard_map/ppermute | solution.py:55
  19.0 5.9 %copy-start.1 = (f32[3]{0:T(128)S(1)}, f32[3]{0:T(128)}, u32[]{:S(2)}) copy-start(f32[3]{0:T(128)} %param.10) | copy-start | bytes 40
  22.9 25.3 %collective-permute-start.10 = (f32[3,128,2048]{2,1,0:T(8,128)}, f32[3,128,2048]{2,1,0:T(8,128)}, u32[]{:S(2)}, u32[]{:S(2)}) collective-permute-start(f32[3,128,2048]{2,1,0:T(8,128)} %dynamic-slice_bitcast_fusion), channel_id=1, source_target_pairs={{0,4},{4,0},{8,12},{12,8},{16,20},{20,16},{24,28},{28,24},{32,36},... | collective-permute-start | bytes 9437192 | tf_op jit(solution)/shard_map/ppermute | solution.py:55
  25.6 6.5 %collective-permute-start.1 = (f32[3,3,4,1792]{3,2,1,0:T(4,128)S(1)}, f32[3,3,4,1792]{3,2,1,0:T(4,128)S(1)}, u32[]{:S(2)}, u32[]{:S(2)}) collective-permute-start(f32[3,3,4,1792]{3,2,1,0:T(4,128)S(1)} %pad_maximum_fusion.8), channel_id=1, source_target_pairs={{0,8},{4,28},{8,0},{12,20},{16,24},{20,12},{24,16},{28,4},{32,40},... | collective-permute-start | bytes 774152 | tf_op jit(solution)/shard_map/ppermute | solution.py:55
  36.5 10.1 %collective-permute-start.5 = (f16[3,64,1536]{2,1,0:T(8,128)(2,1)S(1)}, f16[3,64,1536]{2,1,0:T(8,128)(2,1)S(1)}, u32[]{:S(2)}, u32[]{:S(2)}) collective-permute-start(f16[3,64,1536]{2,1,0:T(8,128)(2,1)S(1)} %bitcast.156), channel_id=1, source_target_pairs={{0,32},{4,228},{8,40},{12,236},{16,48},{20,244},{24,56},{28,252},{... | collective-permute-start | bytes 1769480 | tf_op jit(solution)/shard_map/ppermute | solution.py:55
  39.4 5.6 %collective-permute-start.2 = (f32[3,3,8,896]{3,2,1,0:T(8,128)S(1)}, f32[3,3,8,896]{3,2,1,0:T(8,128)S(1)}, u32[]{:S(2)}, u32[]{:S(2)}) collective-permute-start(f32[3,3,8,896]{3,2,1,0:T(8,128)S(1)} %maximum_maximum_fusion), channel_id=1, source_target_pairs={{0,24},{4,12},{8,16},{12,4},{16,8},{20,28},{24,0},{28,20},{32,56},... | collective-permute-start | bytes 774152 | tf_op jit(solution)/shard_map/ppermute | solution.py:55
  46.9 12.6 %collective-permute-start.6 = (f16[3,32,1536]{2,1,0:T(8,128)(2,1)S(1)}, f16[3,32,1536]{2,1,0:T(8,128)(2,1)S(1)}, u32[]{:S(2)}, u32[]{:S(2)}) collective-permute-start(f16[3,32,1536]{2,1,0:T(8,128)(2,1)S(1)} %bitcast.158), channel_id=1, source_target_pairs={{0,64},{4,68},{8,72},{12,76},{16,80},{20,84},{24,88},{28,92},{32,9... | collective-permute-start | bytes 884744 | tf_op jit(solution)/shard_map/ppermute | solution.py:55
  53.4 12.1 %collective-permute-start.11 = (f16[3,128,1024]{2,1,0:T(8,128)(2,1)S(1)}, f16[3,128,1024]{2,1,0:T(8,128)(2,1)S(1)}, u32[]{:S(2)}, u32[]{:S(2)}) collective-permute-start(f16[3,128,1024]{2,1,0:T(8,128)(2,1)S(1)} %dynamic-slice_convert_fusion), channel_id=1, source_target_pairs={{0,8},{4,28},{8,0},{12,20},{16,24},{20,12},{24,16},{28,4},{32,40},... | collective-permute-start | bytes 2359304 | tf_op jit(solution)/shard_map/ppermute | solution.py:55
  59.6 8.4 %collective-permute-start.7 = (f16[3,16,1536]{2,1,0:T(8,128)(2,1)S(1)}, f16[3,16,1536]{2,1,0:T(8,128)(2,1)S(1)}, u32[]{:S(2)}, u32[]{:S(2)}) collective-permute-start(f16[3,16,1536]{2,1,0:T(8,128)(2,1)S(1)} %fusion.15), channel_id=1, source_target_pairs={{0,128},{4,132},{8,136},{12,140},{16,144},{20,148},{24,152},{28,15... | collective-permute-start | bytes 442376 | tf_op jit(solution)/shard_map/ppermute | solution.py:55
  65.8 6.7 %collective-permute-start.12 = (f16[3,128,512]{2,1,0:T(8,128)(2,1)S(1)}, f16[3,128,512]{2,1,0:T(8,128)(2,1)S(1)}, u32[]{:S(2)}, u32[]{:S(2)}) collective-permute-start(f16[3,128,512]{2,1,0:T(8,128)(2,1)S(1)} %dynamic-slice_convert_fusion.1), channel_id=1, source_target_pairs={{0,24},{4,12},{8,16},{12,4},{16,8},{20,28},{24,0},{28,20},{32,56},... | collective-permute-start | bytes 1179656 | tf_op jit(solution)/shard_map/ppermute | solution.py:55
  68.0 6.9 %collective-permute-start.8 = (f16[3,16,768]{2,1,0:T(8,128)(2,1)S(1)}, f16[3,16,768]{2,1,0:T(8,128)(2,1)S(1)}, u32[]{:S(2)}, u32[]{:S(2)}) collective-permute-start(f16[3,16,768]{2,1,0:T(8,128)(2,1)S(1)} %dynamic-slice_convert_fusion.5), channel_id=1, source_target_pairs={{0,8},{4,28},{8,0},{12,20},{16,24},{20,12},{24,16},{28,4},{32,40},... | collective-permute-start | bytes 221192 | tf_op jit(solution)/shard_map/ppermute | solution.py:55
  72.8 5.8 %collective-permute-start.13 = (f16[3,64,512]{2,1,0:T(8,128)(2,1)S(1)}, f16[3,64,512]{2,1,0:T(8,128)(2,1)S(1)}, u32[]{:S(2)}, u32[]{:S(2)}) collective-permute-start(f16[3,64,512]{2,1,0:T(8,128)(2,1)S(1)} %bitcast.161), channel_id=1, source_target_pairs={{0,32},{4,228},{8,40},{12,236},{16,48},{20,244},{24,56},{28,252},{... | collective-permute-start | bytes 589832 | tf_op jit(solution)/shard_map/ppermute | solution.py:55
  78.7 5.0 %collective-permute-start.14 = (f16[3,32,512]{2,1,0:T(8,128)(2,1)S(1)}, f16[3,32,512]{2,1,0:T(8,128)(2,1)S(1)}, u32[]{:S(2)}, u32[]{:S(2)}) collective-permute-start(f16[3,32,512]{2,1,0:T(8,128)(2,1)S(1)} %bitcast.168), channel_id=1, source_target_pairs={{0,64},{4,68},{8,72},{12,76},{16,80},{20,84},{24,88},{28,92},{32,9... | collective-permute-start | bytes 294920 | tf_op jit(solution)/shard_map/ppermute | solution.py:55
  81.6 6.0 %collective-permute-start.9 = (f16[3,16,384]{2,1,0:T(8,128)(2,1)S(1)}, f16[3,16,384]{2,1,0:T(8,128)(2,1)S(1)}, u32[]{:S(2)}, u32[]{:S(2)}) collective-permute-start(f16[3,16,384]{2,1,0:T(8,128)(2,1)S(1)} %dynamic-slice_convert_fusion.7), channel_id=1, source_target_pairs={{0,24},{4,12},{8,16},{12,4},{16,8},{20,28},{24,0},{28,20},{32,56},... | collective-permute-start | bytes 110600 | tf_op jit(solution)/shard_map/ppermute | solution.py:55
  83.8 7.5 %collective-permute-start.15 = (f16[3,16,512]{2,1,0:T(8,128)(2,1)S(1)}, f16[3,16,512]{2,1,0:T(8,128)(2,1)S(1)}, u32[]{:S(2)}, u32[]{:S(2)}) collective-permute-start(f16[3,16,512]{2,1,0:T(8,128)(2,1)S(1)} %fusion.21), channel_id=1, source_target_pairs={{0,128},{4,132},{8,136},{12,140},{16,144},{20,148},{24,152},{28,15... | collective-permute-start | bytes 147464 | tf_op jit(solution)/shard_map/ppermute | solution.py:55
  91.8 6.3 %collective-permute-start.19 = (bf16[3,16,384]{2,1,0:T(8,128)(2,1)S(1)}, bf16[3,16,384]{2,1,0:T(8,128)(2,1)S(1)}, u32[]{:S(2)}, u32[]{:S(2)}) collective-permute-start(bf16[3,16,384]{2,1,0:T(8,128)(2,1)S(1)} %slice.131), channel_id=1, source_target_pairs={{0,24},{4,12},{8,16},{12,4},{16,8},{20,28},{24,0},{28,20},{32,56},... | collective-permute-start | bytes 110600 | tf_op jit(solution)/shard_map/ppermute | solution.py:55
  91.9 7.2 %collective-permute-start.24 = (bf16[3,16,512]{2,1,0:T(8,128)(2,1)S(1)}, bf16[3,16,512]{2,1,0:T(8,128)(2,1)S(1)}, u32[]{:S(2)}, u32[]{:S(2)}) collective-permute-start(bf16[3,16,512]{2,1,0:T(8,128)(2,1)S(1)} %slice.132), channel_id=1, source_target_pairs={{0,128},{4,132},{8,136},{12,140},{16,144},{20,148},{24,152},{28,15... | collective-permute-start | bytes 147464 | tf_op jit(solution)/shard_map/ppermute | solution.py:55
  95.3 13.7 %collective-permute-start.16 = (f32[3,3,8,896]{3,2,1,0:T(8,128)S(1)}, f32[3,3,8,896]{3,2,1,0:T(8,128)S(1)}, u32[]{:S(2)}, u32[]{:S(2)}) collective-permute-start(f32[3,3,8,896]{3,2,1,0:T(8,128)S(1)} %pad_maximum_fusion.9), channel_id=1, source_target_pairs={{0,8},{4,28},{8,0},{12,20},{16,24},{20,12},{24,16},{28,4},{32,40},... | collective-permute-start | bytes 774152 | tf_op jit(solution)/shard_map/ppermute | solution.py:55
  98.1 4.5 %collective-permute-start.20 = (bf16[3,16,768]{2,1,0:T(8,128)(2,1)S(1)}, bf16[3,16,768]{2,1,0:T(8,128)(2,1)S(1)}, u32[]{:S(2)}, u32[]{:S(2)}) collective-permute-start(bf16[3,16,768]{2,1,0:T(8,128)(2,1)S(1)} %pad_maximum_fusion.17), channel_id=1, source_target_pairs={{0,8},{4,28},{8,0},{12,20},{16,24},{20,12},{24,16},{28,4},{32,40},... | collective-permute-start | bytes 221192 | tf_op jit(solution)/shard_map/ppermute | solution.py:55
  99.1 5.7 %collective-permute-start.25 = (bf16[3,32,512]{2,1,0:T(8,128)(2,1)S(1)}, bf16[3,32,512]{2,1,0:T(8,128)(2,1)S(1)}, u32[]{:S(2)}, u32[]{:S(2)}) collective-permute-start(bf16[3,32,512]{2,1,0:T(8,128)(2,1)S(1)} %bitcast.166), channel_id=1, source_target_pairs={{0,64},{4,68},{8,72},{12,76},{16,80},{20,84},{24,88},{28,92},{32,9... | collective-permute-start | bytes 294920 | tf_op jit(solution)/shard_map/ppermute | solution.py:55
  102.6 11.7 %collective-permute-start.21 = (bf16[3,16,1536]{2,1,0:T(8,128)(2,1)S(1)}, bf16[3,16,1536]{2,1,0:T(8,128)(2,1)S(1)}, u32[]{:S(2)}, u32[]{:S(2)}) collective-permute-start(bf16[3,16,1536]{2,1,0:T(8,128)(2,1)S(1)} %pad_maximum_fusion.15), channel_id=1, source_target_pairs={{0,128},{4,132},{8,136},{12,140},{16,144},{20,148},{24,152},{28,15... | collective-permute-start | bytes 442376 | tf_op jit(solution)/shard_map/ppermute | solution.py:55
  104.9 9.7 %collective-permute-start.26 = (bf16[3,64,512]{2,1,0:T(8,128)(2,1)S(1)}, bf16[3,64,512]{2,1,0:T(8,128)(2,1)S(1)}, u32[]{:S(2)}, u32[]{:S(2)}) collective-permute-start(bf16[3,64,512]{2,1,0:T(8,128)(2,1)S(1)} %bitcast.151), channel_id=1, source_target_pairs={{0,32},{4,228},{8,40},{12,236},{16,48},{20,244},{24,56},{28,252},{... | collective-permute-start | bytes 589832 | tf_op jit(solution)/shard_map/ppermute | solution.py:55
  109.1 5.8 %collective-permute-start.17 = (f32[3,3,8,896]{3,2,1,0:T(8,128)S(1)}, f32[3,3,8,896]{3,2,1,0:T(8,128)S(1)}, u32[]{:S(2)}, u32[]{:S(2)}) collective-permute-start(f32[3,3,8,896]{3,2,1,0:T(8,128)S(1)} %pad_maximum_fusion.10), channel_id=1, source_target_pairs={{0,24},{4,12},{8,16},{12,4},{16,8},{20,28},{24,0},{28,20},{32,56},... | collective-permute-start | bytes 774152 | tf_op jit(solution)/shard_map/ppermute | solution.py:55
  114.4 9.1 %collective-permute-start.22 = (bf16[3,32,1536]{2,1,0:T(8,128)(2,1)S(1)}, bf16[3,32,1536]{2,1,0:T(8,128)(2,1)S(1)}, u32[]{:S(2)}, u32[]{:S(2)}) collective-permute-start(bf16[3,32,1536]{2,1,0:T(8,128)(2,1)S(1)} %bitcast.159), channel_id=1, source_target_pairs={{0,64},{4,68},{8,72},{12,76},{16,80},{20,84},{24,88},{28,92},{32,9... | collective-permute-start | bytes 884744 | tf_op jit(solution)/shard_map/ppermute | solution.py:55
  114.7 27.0 %collective-permute-start.27 = (bf16[3,128,512]{2,1,0:T(8,128)(2,1)S(1)}, bf16[3,128,512]{2,1,0:T(8,128)(2,1)S(1)}, u32[]{:S(2)}, u32[]{:S(2)}) collective-permute-start(bf16[3,128,512]{2,1,0:T(8,128)(2,1)S(1)} %bitcast.148), channel_id=1, source_target_pairs={{0,24},{4,12},{8,16},{12,4},{16,8},{20,28},{24,0},{28,20},{32,56},... | collective-permute-start | bytes 1179656 | tf_op jit(solution)/shard_map/ppermute | solution.py:55
  123.7 18.2 %collective-permute-start.23 = (bf16[3,64,1536]{2,1,0:T(8,128)(2,1)S(1)}, bf16[3,64,1536]{2,1,0:T(8,128)(2,1)S(1)}, u32[]{:S(2)}, u32[]{:S(2)}) collective-permute-start(bf16[3,64,1536]{2,1,0:T(8,128)(2,1)S(1)} %bitcast.144), channel_id=1, source_target_pairs={{0,32},{4,228},{8,40},{12,236},{16,48},{20,244},{24,56},{28,252},{... | collective-permute-start | bytes 1769480 | tf_op jit(solution)/shard_map/ppermute | solution.py:55
  131.6 23.2 %collective-permute-start.18 = (f32[3,3,2,3584]{3,2,1,0:T(2,128)S(1)}, f32[3,3,2,3584]{3,2,1,0:T(2,128)S(1)}, u32[]{:S(2)}, u32[]{:S(2)}) collective-permute-start(f32[3,3,2,3584]{3,2,1,0:T(2,128)S(1)} %constant_dynamic-slice_fusion), channel_id=1, source_target_pairs={{0,4},{4,0},{8,12},{12,8},{16,20},{20,16},{24,28},{28,24},{32,36},... | collective-permute-start | bytes 774152 | tf_op jit(solution)/shard_map/ppermute | solution.py:55
  141.9 12.1 %collective-permute-start.28 = (bf16[3,128,1024]{2,1,0:T(8,128)(2,1)S(1)}, bf16[3,128,1024]{2,1,0:T(8,128)(2,1)S(1)}, u32[]{:S(2)}, u32[]{:S(2)}) collective-permute-start(bf16[3,128,1024]{2,1,0:T(8,128)(2,1)S(1)} %pad_maximum_fusion.2), channel_id=1, source_target_pairs={{0,8},{4,28},{8,0},{12,20},{16,24},{20,12},{24,16},{28,4},{32,40},... | collective-permute-start | bytes 2359304 | tf_op jit(solution)/shard_map/ppermute | solution.py:55
  142.4 13.6 %collective-permute-start.29 = (bf16[3,128,1536]{2,1,0:T(8,128)(2,1)S(1)}, bf16[3,128,1536]{2,1,0:T(8,128)(2,1)S(1)}, u32[]{:S(2)}, u32[]{:S(2)}) collective-permute-start(bf16[3,128,1536]{2,1,0:T(8,128)(2,1)S(1)} %bitcast.140), channel_id=1, source_target_pairs={{0,4},{4,0},{8,12},{12,8},{16,20},{20,16},{24,28},{28,24},{32,36},... | collective-permute-start | bytes 3538952 | tf_op jit(solution)/shard_map/ppermute | solution.py:55
  154.7 3.5 %collective-permute-start.30 = (bf16[3,128,2048]{2,1,0:T(8,128)(2,1)S(1)}, bf16[3,128,2048]{2,1,0:T(8,128)(2,1)S(1)}, u32[]{:S(2)}, u32[]{:S(2)}) collective-permute-start(bf16[3,128,2048]{2,1,0:T(8,128)(2,1)S(1)} %get-tuple-element.9), channel_id=1, source_target_pairs={{0,4},{4,0},{8,12},{12,8},{16,20},{20,16},{24,28},{28,24},{32,36},... | collective-permute-start | bytes 4718600 | tf_op jit(solution)/shard_map/ppermute | solution.py:55
  158.4 2.5 %copy-start = (bf16[3,128,7168]{2,1,0:T(8,128)(2,1)}, bf16[3,128,7168]{2,1,0:T(8,128)(2,1)S(1)}, u32[]{:S(2)}) copy-start(bf16[3,128,7168]{2,1,0:T(8,128)(2,1)S(1)} %constant_dynamic-update-slice_fusion) | copy-start | bytes 16515076

commit v2 on v0

v2 whole, which is shorter than its diff:
```python
import jax
import jax.numpy as jnp
from jax import lax
from jax.experimental import pallas as pl
from jax.experimental.pallas import tpu as pltpu
from jax.sharding import Mesh
from jax.sharding import PartitionSpec as P

DP = ("z", "x", "c")
DEEP, WIDE = 8, 4

beta_one = 0.9
beta_two = 0.95
bias_one = 1.0 - 0.9**10
bias_two = 1.0 - 0.95**10
epsilon = 1e-08
learn_rate = 0.01
decay_rate = 0.1

RAISE = 4.0
LINK = jnp.float16


def adam_update(grad_sum, first, second, weights):
    first_new = beta_one * first + (1.0 - beta_one) * grad_sum
    second_new = beta_two * second + (1.0 - beta_two) * grad_sum * grad_sum
    step_size = first_new / bias_one / (jnp.sqrt(second_new / bias_two) + epsilon)
    weights_new = weights - learn_rate * (step_size + decay_rate * weights)
    return (weights_new, first_new, second_new)


def x_partner(step, z, x, c):
    return (z, x ^ (1 if step == c else 3), c)


def z_partner(step, z, x, c):
    return ((((z + c) % DEEP) ^ 1) - c) % DEEP, x, c


def z_ahead(step, z, x, c):
    return (z + 2 * step) % DEEP, x, c


def core_partner(step, z, x, c):
    return (z, x, 1 - c)


def trade(value, partner, step=0):
    def index(z, x, c):
        return (z * WIDE + x) * 2 + c

    perm = [
        (index(z, x, c), index(*partner(step, z, x, c)))
        for z in range(DEEP)
        for x in range(WIDE)
        for c in range(2)
    ]
    return lax.ppermute(value, DP, perm)


def x_bits(x, c):
    high, mixed = x // 2, (x + x // 2) % 2
    return (mixed * (1 - c) + high * c, high * (1 - c) + mixed * c)


def pick(value, index, parts, dim):
    size = value.shape[dim] // parts
    return lax.dynamic_slice_in_dim(value, index * size, size, dim)


def send(value, partner, step):
    return trade(value.astype(LINK), partner, step).astype(jnp.float32)


def both(own, got, bit, dim):
    first = jnp.where(bit == 0, own, got)
    second = jnp.where(bit == 0, got, own)
    return jnp.concatenate([first, second], axis=dim)


def pick_z(value, index):
    mats, blocks, *rest = value.shape
    pairs = value.reshape(mats, blocks // 2, 2, *rest)
    return lax.dynamic_slice_in_dim(pairs, index, 1, 2).reshape(mats, blocks // 2, *rest)


def sum_x(value, bits, step):
    got = send(pick(value, 1 - bits[step], 2, 3), x_partner, step)
    return pick(value, bits[step], 2, 3) + got


def sum_z(value, odd):
    got = send(pick_z(value, 1 - odd), z_partner, 0)
    return pick_z(value, odd) + got


FAR = (2, 1, 3)


def sum_quad(value, place):
    got = [send(pick(value, (place + k) % 4, 4, 1), z_ahead, k) for k in FAR]
    return pick(value, place, 4, 1) + got[0] + got[1] + got[2]


def gather_quad(value, place):
    mats, _, *rest = value.shape
    got = [trade(value, z_ahead, k) for k in FAR]
    whole = jnp.zeros((mats, 4, *rest), value.dtype)
    for k, piece in zip((0, *FAR), (value, *got)):
        whole = lax.dynamic_update_slice_in_dim(whole, piece, (place - k) % 4, 1)
    return whole


def gather_x(value, bits, step):
    return both(value, trade(value, x_partner, step), bits[step], 3)


def gather_z(value, odd):
    mats, blocks, *rest = value.shape
    got = trade(value, z_partner, 0)
    own, got = (v.reshape(mats, blocks, 1, *rest) for v in (value, got))
    return both(own, got, odd, 2).reshape(mats, 2 * blocks, *rest)


def x_places(across, mine):
    masks = (1 + 2 * mine, 3 - 2 * mine)
    return (across, across ^ masks[0], across ^ masks[1], across ^ masks[0] ^ masks[1])


def split_step(groups, bits, step):
    give = jnp.concatenate([pick(v, 1 - bits[step], 2, 3) for v in groups], axis=2)
    got = trade(give, x_partner, step)
    groups = [pick(v, bits[step], 2, 3) for v in groups]
    return groups + [got[:, :, 4 * k : 4 * k + 4] for k in range(len(groups))]


def rows_in_order(groups, across, mine):
    one = groups[0]
    whole = jnp.zeros((*one.shape[:2], 16, one.shape[3]), one.dtype)
    for place, group in zip(x_places(across, mine), groups):
        whole = lax.dynamic_update_slice_in_dim(whole, group, 4 * place, 2)
    return whole


def join_columns(state, across, mine, bits):
    own, one, two, three = [pick(state, place, 4, 2) for place in x_places(across, mine)]
    got = trade(jnp.concatenate([one, three], axis=2), x_partner, 0)
    first = got[:, :, :4]
    got = trade(jnp.concatenate([two, got[:, :, 4:]], axis=2), x_partner, 1)
    place, width = 2 * bits[0] + bits[1], state.shape[3]
    left = jnp.zeros((*state.shape[:2], 4, 4 * width), state.dtype)
    for chunk, flip in zip((own, first, got[:, :, :4], got[:, :, 4:]), (0, 2, 1, 3)):
        left = lax.dynamic_update_slice_in_dim(left, chunk, width * (place ^ flip), 3)
    return left


def scale_kernel(at_ref, notes_ref, weight_ref, own_ref, raw_ref):
    totals = jnp.sum(notes_ref[...], axis=0).astype(jnp.float32)
    ratios = weight_ref[...] / totals
    lanes = lax.broadcasted_iota(jnp.int32, ratios.shape, 1)
    for j, out in enumerate((own_ref, raw_ref)):
        kind = notes_ref[at_ref[j]][:, 3:4]
        picked = jnp.sum(jnp.where(lanes == kind, ratios, 0.0), axis=1, keepdims=True)
        out[...] = jnp.broadcast_to(picked * RAISE, out.shape)


def scale_rows(notes, loss_weight, places, width):
    weight = jnp.pad(loss_weight, (0, 1))[None]
    return pl.pallas_call(
        scale_kernel,
        out_shape=[jax.ShapeDtypeStruct((1, width), jnp.float32)] * 2,
        in_specs=[
            pl.BlockSpec(memory_space=pltpu.SMEM),
            pl.BlockSpec(memory_space=pltpu.VMEM),
            pl.BlockSpec(memory_space=pltpu.VMEM),
        ],
        out_specs=[pl.BlockSpec(memory_space=pltpu.VMEM)] * 2,
        compiler_params=pltpu.CompilerParams(vmem_limit_bytes=1 << 20),
    )(places, notes, weight)


def local(gradients, token_counts, modality, loss_weight, master, moment_one, moment_two):
    mats, rows, cols = 3, gradients.shape[1], gradients.shape[3]
    half = cols // 2
    depth, across, mine = (lax.axis_index(a) for a in DP)
    odd, place = depth % 2, depth // 2
    xb = x_bits(across, mine)

    notes = jnp.concatenate([token_counts, modality[:, None]], axis=1)
    notes = jnp.broadcast_to(notes, (DEEP * WIDE * 2, 4))[:, None]
    notes = lax.all_to_all(notes, DP, 0, 0, tiled=True)

    grad = jnp.transpose(gradients[0], (1, 0, 2)).reshape(mats, DEEP, 2, 8, cols)

    def tile(grad, t, core):
        cut = lax.dynamic_slice(grad, (0, 0, t, 0, core * half), (mats, DEEP, 1, 8, half))
        return cut.reshape(mats, DEEP, 8, half)

    give_a = tile(grad, 0, 1 - mine)
    grad, give_a = lax.optimization_barrier((grad, give_a))
    give_b = tile(grad, 1, 1 - mine)
    grad, give_b = lax.optimization_barrier((grad, give_b))
    own = [tile(grad, t, mine) for t in range(2)]
    raw_a = trade(give_a, core_partner)
    raw_b = trade(give_b, core_partner)
    raw = [raw_a, raw_b]

    state = jnp.stack([jnp.transpose(a, (1, 0, 2)) for a in (master, moment_one, moment_two)])
    got = trade(pick(state, 1 - mine, 2, 3), core_partner)
    state = both(pick(state, mine, 2, 3), got, mine, 2)

    chip = 2 * (WIDE * depth + across)
    scales = scale_rows(notes, loss_weight, jnp.stack([chip + mine, chip + 1 - mine]), half)

    def combined(t, cut):
        wide = cut(own[t])
        first, second = (scale[:, : wide.shape[3]] for scale in scales)
        return wide * first + cut(raw[t]) * second

    give_a = combined(0, lambda v: pick_z(v, 1 - odd)).astype(LINK)
    give_b = combined(1, lambda v: pick(v, 1 - xb[0], 2, 3)).astype(LINK)
    raw_a, give_a = lax.optimization_barrier((raw[0], give_a))
    raw_b, give_b = lax.optimization_barrier((raw[1], give_b))
    raw = [raw_a, raw_b]
    part_a = lax.optimization_barrier(combined(0, lambda v: pick_z(v, odd)))
    part_b = lax.optimization_barrier(combined(1, lambda v: pick(v, xb[0], 2, 3)))
    got_a = send(give_a, z_partner, 0)
    got_b = send(give_b, x_partner, 0)
    part_a, part_b = part_a + got_a, part_b + got_b
    part_a = sum_x(part_a, xb, 0)
    part_b = sum_z(part_b, odd)
    groups = split_step([state], xb, 0)
    part = jnp.concatenate([part_a, part_b], axis=2)
    give_c = pick(part, 1 - xb[1], 2, 3).astype(LINK)
    got = trade(give_c, x_partner, 1)
    groups = split_step(groups, xb, 1)
    part = lax.optimization_barrier(pick(part, xb[1], 2, 3) + got.astype(jnp.float32))

    state = rows_in_order(groups, across, mine)

    summed = sum_quad(part, place)[:, 0] * (1.0 / RAISE)
    new = adam_update(summed, state[1], state[2], state[0])
    lean = new[0].astype(jnp.bfloat16)[:, None]

    lean = gather_quad(lean, place)
    lean = gather_x(lean, xb, 1)
    lean_a = gather_x(lean[:, :, :8], xb, 0)
    lean_b = gather_z(lean[:, :, 8:], odd)
    got_a, got_b = trade(lean_a, z_partner), trade(lean_b, x_partner, 0)
    whole = jnp.zeros((mats, DEEP // 2, 2, 2, 8, cols), jnp.bfloat16)
    for core in (mine, 1 - mine):
        side = x_bits(across, core)[0]
        for tile_a, tile_b, place_a, place_b in (
            (lean_a, lean_b, odd, side),
            (got_a, got_b, 1 - odd, 1 - side),
        ):
            if core is not mine:
                tile_a, tile_b = trade(tile_a, core_partner), trade(tile_b, core_partner)
            tile_a = tile_a[:, :, None, None]
            whole = lax.dynamic_update_slice(whole, tile_a, (0, 0, place_a, 0, 0, core * half))
            tile_b = tile_b.reshape(mats, DEEP // 2, 2, 1, 8, half // 2)
            at = core * half + place_b * (half // 2)
            whole = lax.dynamic_update_slice(whole, tile_b, (0, 0, 0, 1, 0, at))
    whole = whole.reshape(mats, rows, cols)

    left = join_columns(jnp.stack(new), across, mine, xb)
    back = both(pick(left, mine, 2, 2), trade(pick(left, 1 - mine, 2, 2), core_partner), mine, 3)
    outs = [jnp.transpose(back[i], (1, 0, 2)) for i in range(3)]
    return (*outs, jnp.transpose(whole, (1, 0, 2)))


def solution(mesh):
    torus = Mesh(mesh.devices.reshape(DEEP, WIDE, 2, mesh.shape["tensor"]), (*DP, "tensor"))
    in_specs = (
        P(DP, None, None, "tensor"),
        P(DP, None),
        P(DP),
        P(),
        P(DP, None, "tensor"),
        P(DP, None, "tensor"),
        P(DP, None, "tensor"),
    )
    out_specs = (
        P(DP, None, "tensor"),
        P(DP, None, "tensor"),
        P(DP, None, "tensor"),
        P(None, None, "tensor"),
    )

    return jax.shard_map(local, mesh=torus, in_specs=in_specs, out_specs=out_specs, check_vma=False)
```

time: 352 us -> 137 us (0.39)
  waiting for transfers between devices: 274 us -> 40.3 us
  starting transfers between devices: 13.2 us -> 60.5 us
  between operations: 15.8 us -> 1.83 us
  blocking collectives: 10.5 us -> 0 us
  local copies, waits for them, and re-layouts: 23.7 us -> 16.1 us
    reduce_scatter x1 -> x0, waiting for transfers between devices: 114 us -> none  [scatter_axes(): nearer = lax.psum_scatter(value, axes[0], scatter_dimension=dim, tiled=True)]
    unnamed x7 -> x0, waiting for transfers between devices: 83.4 us -> none
    all_gather x2 -> x0, waiting for transfers between devices: 67.7 us -> none  [all_blocks(): parts = lax.all_gather(parts, axes[k], axis=0, tiled=True)]
    ppermute x0 -> x28, starting transfers between devices: none -> 50.2 us  [trade(): return lax.ppermute(value, DP, perm)]
    ppermute x0 -> x28, waiting for transfers between devices: none -> 40.3 us  [trade(): return lax.ppermute(value, DP, perm)]
    another operation x1, local copies, waits for them, and re-layouts: 11.8 us -> 0.64 us  [local(): notes = jnp.broadcast_to(notes, (DEEP * WIDE * 2, 4))[:, None]]
    all_gather x1 -> x0, blocking collectives: 10.5 us -> none  [all_blocks(): parts = lax.all_gather(parts, axes[k], axis=0, tiled=True)]
    mul x1 -> x0, other arithmetic: 10.2 us -> none  [local(): summed = scatter_axes(replica_grad * own_scale, DP, 0)]
  transfers between devices with their start and end apart: 6 -> 29, of which waited for: 6 -> 15; matrix products, arithmetic and copies ran while one was open for 0% -> 21% of each run, Pallas kernels for 0% -> 1%
where the time goes in v2:
time: 137 us; the launch traced here: 136 us
  starting transfers between devices  60.5 us (44%)
  waiting for transfers between devices  40.3 us (29%)
  other arithmetic  16.9 us (12%)
  local copies, waits for them, and re-layouts  16.1 us (12%)
  between operations  1.83 us (1%)
    ppermute x28, starting transfers between devices, trade(): return lax.ppermute(value, DP, perm)  50.2 us
    ppermute x28, waiting for transfers between devices, trade(): return lax.ppermute(value, DP, perm)  40.3 us
    all_to_all x1, starting transfers between devices, local(): notes = lax.all_to_all(notes, DP, 0, 0, tiled=True)  10.3 us
    reshape x2, local copies, waits for them, and re-layouts, tile(): return cut.reshape(mats, DEEP, 8, half)  7.01 us
    add x2, other arithmetic, combined(): return wide * first + cut(raw[t]) * second  3.76 us
    unnamed x12, local copies, waits for them, and re-layouts  3.32 us
  transfers between devices with their start and end apart: 29, of which 15 were waited for; matrix products, arithmetic and copies ran while one was open for 21% of the time, Pallas kernels for 1%

profile of v2, /device:TPU:1, one launch (start us, length us, event | category | flops | bytes accessed | tf_op | source)
XLA Modules:
  0.0 136.4 jit_solution(2895873575751116639)
XLA Ops:
  0.6 1.3 pad_maximum_fusion.2
  2.0 0.9 copy-done.2
  2.8 3.3 %collective-permute-start = (f32[3,3,2,3584]{3,2,1,0:T(2,128)S(1)}, f32[3,3,2,3584]{3,2,1,0:T(2,128)}, u32[]{:S(2)}, u32[]{:S(2)}) collective-permute-start(f32[3,3,2,3584]{3,2,1,0:T(2,128)S(1)} %constant_dynamic-slice_fusion.6), channel_id=1, source_target_pairs={{0,4},{4,0},{8,12},{12,8},{16,20},{20,16},{24,28},{28,24},{32,36},... | collective-permute-start | bytes 774152 | tf_op jit(solution)/shard_map/ppermute | solution.py:58
  6.1 3.5 %dynamic-slice_bitcast_fusion.1 = f32[3,8,8,3584]{3,2,1,0:T(8,128)} fusion(f32[3,8,2,8,7168]{4,3,2,1,0:T(8,128)} %bitcast.170, s32[]{:T(128)S(6)} %select_n.249), kind=kLoop, calls=%fused_computation.1 | loop fusion | bytes 5505028 | tf_op jit(solution)/shard_map/reshape | solution.py:197
  11.0 10.3 %all-to-all-start = ((s32[64,1,4]{2,1,0:T(1,128)}), s32[64,1,4]{2,1,0:T(1,128)S(1)}, u32[]{:S(2)}, u32[]{:S(2)}) async-start(s32[64,1,4]{2,1,0:T(1,128)} %broadcast_in_dim_broadcast_in_dim.2), calls=%async_computation | async-start | bytes 65536 | tf_op jit(solution)/shard_map/all_to_all | solution.py:191
  21.3 3.5 %dynamic-slice_bitcast_fusion = f32[3,8,8,3584]{3,2,1,0:T(8,128)} fusion(f32[3,8,2,8,7168]{4,3,2,1,0:T(8,128)} %bitcast.171, s32[]{:T(128)S(6)} %select_n.249), kind=kLoop, calls=%fused_computation | loop fusion | bytes 5505028 | tf_op jit(solution)/shard_map/reshape | solution.py:197
  25.3 2.0 %constant_dynamic-slice_fusion.4 = f32[3,8,1,8,3584]{4,3,2,1,0:T(8,128)S(1)} fusion(f32[3,8,2,8,7168]{4,3,2,1,0:T(8,128)} %bitcast.172, s32[]{:T(128)S(6)} %select_n.248), kind=kLoop, calls=%fused_computation.115 | loop fusion | bytes 5505028 | tf_op jit(solution)/shard_map/dynamic_slice | solution.py:196
  27.3 1.3 broadcast_select_fusion.6
  28.6 0.9 fusion.12
  29.5 2.5 %collective-permute-start.1 = (f32[3,3,4,1792]{3,2,1,0:T(4,128)}, f32[3,3,4,1792]{3,2,1,0:T(4,128)}, u32[]{:S(2)}, u32[]{:S(2)}) collective-permute-start(f32[3,3,4,1792]{3,2,1,0:T(4,128)} %fusion.12), channel_id=1, source_target_pairs={{0,8},{4,28},{8,0},{12,20},{16,24},{20,12},{24,16},{28,4},{32,40},... | collective-permute-start | bytes 774152 | tf_op jit(solution)/shard_map/ppermute | solution.py:58
  33.6 1.4 %fusion.27 = (f32[3,3,4,896]{3,2,1,0:T(4,128)S(1)}, f32[3,3,16,896]{3,2,1,0:T(8,128)S(1)}) fusion(s32[]{:T(128)S(6)} %dynamic_slice.124, f32[3,3,2,3584]{3,2,1,0:T(2,128)} %copy-done.1, f32[3,3,2,3584]{3,2,1,0:T(2,128)S(1)} %get-tuple-element.32, f32[3,3,16,896]{3,2,1,0:T(8,128)S(1)} %broadcast_in_dim.40, s32[]{:T(128)S(6)} %select_n.258, s32[]{:T(128)S(6)} %dynamic_slice.120), kind=kLoop, calls=%fused_computation.95 | loop fusion | flops 64512 | bytes 774156 | tf_op jit(solution)/shard_map/concatenate | solution.py:78
  35.0 1.2 collective-permute-done.1
  36.2 1.0 constant_dynamic-slice_fusion.5
  38.4 1.6 %fusion.5 = f16[3,4,8,3584]{3,2,1,0:T(8,128)(2,1)S(1)} fusion(f32[3,4,2,8,3584]{4,3,2,1,0:T(8,128)} %bitcast.21, s32[]{:T(128)S(6)} %select_n.267, f32[3,4,2,8,3584]{4,3,2,1,0:T(8,128)S(1)} %bitcast.175, f32[3584]{0:T(1024)S(1)} %reduce.1, f32[3584]{0:T(1024)S(1)} %copy-done.3), kind=kLoop, calls=%fused_computation.15 | loop fusion | flops 1376256 | bytes 3469316 | tf_op jit(solution)/shard_map/convert_element_type | solution.py:220
  40.0 2.8 %collective-permute-start.4 = (f16[3,4,8,3584]{3,2,1,0:T(8,128)(2,1)S(1)}, f16[3,4,8,3584]{3,2,1,0:T(8,128)(2,1)S(1)}, u32[]{:S(2)}, u32[]{:S(2)}) collective-permute-start(f16[3,4,8,3584]{3,2,1,0:T(8,128)(2,1)S(1)} %fusion.5), channel_id=1, source_target_pairs={{0,32},{4,228},{8,40},{12,236},{16,48},{20,244},{24,56},{28,252},{... | collective-permute-start | bytes 2064392 | tf_op jit(solution)/shard_map/ppermute | solution.py:58
  42.7 1.5 %fusion.3 = f32[3,4,8,3584]{3,2,1,0:T(8,128)S(1)} fusion(f32[3,4,2,8,3584]{4,3,2,1,0:T(8,128)} %bitcast.23, s32[]{:T(128)S(6)} %select_n.266, f32[3,4,2,8,3584]{4,3,2,1,0:T(8,128)S(1)} %bitcast.176, f32[3584]{0:T(1024)S(1)} %reduce.1, f32[3584]{0:T(1024)S(1)} %copy-done.3), kind=kLoop, calls=%fused_computation.12 | loop fusion | flops 1032192 | bytes 4157444 | tf_op jit(solution)/shard_map/add | solution.py:218
  44.3 2.2 %fusion.1 = f16[3,8,8,1792]{3,2,1,0:T(8,128)(2,1)S(1)} fusion(f32[3,8,8,3584]{3,2,1,0:T(8,128)} %collective-permute-done.6, s32[]{:T(128)S(6)} %select_n.259, f32[3,8,2,8,7168]{4,3,2,1,0:T(8,128)} %bitcast.173, s32[]{:T(128)S(6)} %dynamic_slice.139, f32[1792]{0:T(1024)S(1)} %get-tuple-element.58, f32[1792]{0:T(1024)S(1)} %get-tuple-element.59), kind=kLoop, calls=%fused_computation.8 | loop fusion | flops 1376256 | bytes 3454984 | tf_op jit(solution)/shard_map/convert_element_type | solution.py:221
  46.5 2.2 %fusion.2 = f32[3,8,8,1792]{3,2,1,0:T(8,128)S(1)} fusion(f32[3,8,8,3584]{3,2,1,0:T(8,128)} %collective-permute-done.6, s32[]{:T(128)S(6)} %select_n.256, f32[3,8,2,8,7168]{4,3,2,1,0:T(8,128)} %bitcast.174, s32[]{:T(128)S(6)} %dynamic_slice.136, f32[1792]{0:T(1024)S(1)} %get-tuple-element.58, f32[1792]{0:T(1024)S(1)} %get-tuple-element.59), kind=kLoop, calls=%fused_computation.10 | loop fusion | flops 1032192 | bytes 4143112 | tf_op jit(solution)/shard_map/add | solution.py:218
  48.7 2.3 %collective-permute-start.7 = (f16[3,8,8,1792]{3,2,1,0:T(8,128)(2,1)S(1)}, f16[3,8,8,1792]{3,2,1,0:T(8,128)(2,1)S(1)}, u32[]{:S(2)}, u32[]{:S(2)}) collective-permute-start(f16[3,8,8,1792]{3,2,1,0:T(8,128)(2,1)S(1)} %fusion.1), channel_id=1, source_target_pairs={{0,8},{4,28},{8,0},{12,20},{16,24},{20,12},{24,16},{28,4},{32,40},... | collective-permute-start | bytes 2064392 | tf_op jit(solution)/shard_map/ppermute | solution.py:58
  51.3 2.3 %collective-permute-start.5 = (f16[3,4,8,1792]{3,2,1,0:T(8,128)(2,1)S(1)}, f16[3,4,8,1792]{3,2,1,0:T(8,128)(2,1)S(1)}, u32[]{:S(2)}, u32[]{:S(2)}) collective-permute-start(f16[3,4,8,1792]{3,2,1,0:T(8,128)(2,1)S(1)} %dynamic-slice_convert_fusion.1), channel_id=1, source_target_pairs={{0,8},{4,28},{8,0},{12,20},{16,24},{20,12},{24,16},{28,4},{32,40},... | collective-permute-start | bytes 1032200 | tf_op jit(solution)/shard_map/ppermute | solution.py:58
  53.5 6.3 %collective-permute-done.7 = f16[3,8,8,1792]{3,2,1,0:T(8,128)(2,1)S(1)} collective-permute-done((f16[3,8,8,1792]{3,2,1,0:T(8,128)(2,1)S(1)}, f16[3,8,8,1792]{3,2,1,0:T(8,128)(2,1)S(1)}, u32[]{:S(2)}, u32[]{:S(2)}) %collective-permute-start.7) | collective-permute-done | bytes 688160 | tf_op jit(solution)/shard_map/ppermute | solution.py:58
  60.1 3.4 %collective-permute-done.5 = f16[3,4,8,1792]{3,2,1,0:T(8,128)(2,1)S(1)} collective-permute-done((f16[3,4,8,1792]{3,2,1,0:T(8,128)(2,1)S(1)}, f16[3,4,8,1792]{3,2,1,0:T(8,128)(2,1)S(1)}, u32[]{:S(2)}, u32[]{:S(2)}) %collective-permute-start.5) | collective-permute-done | bytes 344096 | tf_op jit(solution)/shard_map/ppermute | solution.py:58
  63.6 3.8 %collective-permute-done.8 = f16[3,4,8,1792]{3,2,1,0:T(8,128)(2,1)S(1)} collective-permute-done((f16[3,4,8,1792]{3,2,1,0:T(8,128)(2,1)S(1)}, f16[3,4,8,1792]{3,2,1,0:T(8,128)(2,1)S(1)}, u32[]{:S(2)}, u32[]{:S(2)}) %collective-permute-start.8) | collective-permute-done | bytes 344096 | tf_op jit(solution)/shard_map/ppermute | solution.py:58
  68.3 5.7 %collective-permute-done.9 = f16[3,4,16,896]{3,2,1,0:T(8,128)(2,1)S(1)} collective-permute-done((f16[3,4,16,896]{3,2,1,0:T(8,128)(2,1)S(1)}, f16[3,4,16,896]{3,2,1,0:T(8,128)(2,1)S(1)}, u32[]{:S(2)}, u32[]{:S(2)}) %collective-permute-start.9) | collective-permute-done | bytes 344096 | tf_op jit(solution)/shard_map/ppermute | solution.py:58
  74.1 0.8 collective-permute-start.12
  75.0 1.6 %collective-permute-start.11 = (f16[3,1,16,896]{3,2,1,0:T(8,128)(2,1)S(1)}, f16[3,1,16,896]{3,2,1,0:T(8,128)(2,1)S(1)}, u32[]{:S(2)}, u32[]{:S(2)}) collective-permute-start(f16[3,1,16,896]{3,2,1,0:T(8,128)(2,1)S(1)} %get-tuple-element.44), channel_id=1, source_target_pairs={{0,64},{4,68},{8,72},{12,76},{16,80},{20,84},{24,88},{28,92},{32,9... | collective-permute-start | bytes 258056 | tf_op jit(solution)/shard_map/ppermute | solution.py:58
  76.6 2.5 %collective-permute-start.10 = (f16[3,1,16,896]{3,2,1,0:T(8,128)(2,1)S(1)}, f16[3,1,16,896]{3,2,1,0:T(8,128)(2,1)S(1)}, u32[]{:S(2)}, u32[]{:S(2)}) collective-permute-start(f16[3,1,16,896]{3,2,1,0:T(8,128)(2,1)S(1)} %get-tuple-element.42), channel_id=1, source_target_pairs={{0,128},{4,132},{8,136},{12,140},{16,144},{20,148},{24,152},{28,15... | collective-permute-start | bytes 258056 | tf_op jit(solution)/shard_map/ppermute | solution.py:58
  79.1 1.3 collective-permute-done.11
  80.4 4.9 %collective-permute-done.10 = f16[3,1,16,896]{3,2,1,0:T(8,128)(2,1)S(1)} collective-permute-done((f16[3,1,16,896]{3,2,1,0:T(8,128)(2,1)S(1)}, f16[3,1,16,896]{3,2,1,0:T(8,128)(2,1)S(1)}, u32[]{:S(2)}, u32[]{:S(2)}) %collective-permute-start.10) | collective-permute-done | bytes 86048 | tf_op jit(solution)/shard_map/ppermute | solution.py:58
  85.6 1.1 collective-permute-start.16
  86.7 2.6 %collective-permute-start.17 = (bf16[3,1,16,896]{3,2,1,0:T(8,128)(2,1)S(1)}, bf16[3,1,16,896]{3,2,1,0:T(8,128)(2,1)S(1)}, u32[]{:S(2)}, u32[]{:S(2)}) collective-permute-start(bf16[3,1,16,896]{3,2,1,0:T(8,128)(2,1)S(1)} %get-tuple-element.25), channel_id=1, source_target_pairs={{0,64},{4,68},{8,72},{12,76},{16,80},{20,84},{24,88},{28,92},{32,9... | collective-permute-start | bytes 258056 | tf_op jit(solution)/shard_map/ppermute | solution.py:58
  89.3 1.0 collective-permute-start.18
  90.8 3.0 %collective-permute-start.13 = (f32[3,3,8,896]{3,2,1,0:T(8,128)S(1)}, f32[3,3,8,896]{3,2,1,0:T(8,128)S(1)}, u32[]{:S(2)}, u32[]{:S(2)}) collective-permute-start(f32[3,3,8,896]{3,2,1,0:T(8,128)S(1)} %pad_maximum_fusion.6), channel_id=1, source_target_pairs={{0,8},{4,28},{8,0},{12,20},{16,24},{20,12},{24,16},{28,4},{32,40},... | collective-permute-start | bytes 774152 | tf_op jit(solution)/shard_map/ppermute | solution.py:58
  93.8 1.2 collective-permute-done.18
  95.0 0.9 collective-permute-start.19
  95.9 1.9 %collective-permute-done.13 = f32[3,3,8,896]{3,2,1,0:T(8,128)S(1)} collective-permute-done((f32[3,3,8,896]{3,2,1,0:T(8,128)S(1)}, f32[3,3,8,896]{3,2,1,0:T(8,128)S(1)}, u32[]{:S(2)}, u32[]{:S(2)}) %collective-permute-start.13) | collective-permute-done | bytes 258080 | tf_op jit(solution)/shard_map/ppermute | solution.py:58
  98.0 3.2 %collective-permute-done.19 = bf16[3,4,16,896]{3,2,1,0:T(8,128)(2,1)S(1)} collective-permute-done((bf16[3,4,16,896]{3,2,1,0:T(8,128)(2,1)S(1)}, bf16[3,4,16,896]{3,2,1,0:T(8,128)(2,1)S(1)}, u32[]{:S(2)}, u32[]{:S(2)}) %collective-permute-start.19) | collective-permute-done | bytes 344096 | tf_op jit(solution)/shard_map/ppermute | solution.py:58
  101.4 5.8 %collective-permute-start.20 = (bf16[3,4,8,1792]{3,2,1,0:T(8,128)(2,1)S(1)}, bf16[3,4,8,1792]{3,2,1,0:T(8,128)(2,1)S(1)}, u32[]{:S(2)}, u32[]{:S(2)}) collective-permute-start(bf16[3,4,8,1792]{3,2,1,0:T(8,128)(2,1)S(1)} %get-tuple-element.37), channel_id=1, source_target_pairs={{0,8},{4,28},{8,0},{12,20},{16,24},{20,12},{24,16},{28,4},{32,40},... | collective-permute-start | bytes 1032200 | tf_op jit(solution)/shard_map/ppermute | solution.py:58
  107.2 1.8 %collective-permute-start.21 = (bf16[3,4,8,1792]{3,2,1,0:T(8,128)(2,1)S(1)}, bf16[3,4,8,1792]{3,2,1,0:T(8,128)(2,1)S(1)}, u32[]{:S(2)}, u32[]{:S(2)}) collective-permute-start(bf16[3,4,8,1792]{3,2,1,0:T(8,128)(2,1)S(1)} %get-tuple-element.36), channel_id=1, source_target_pairs={{0,32},{4,228},{8,40},{12,236},{16,48},{20,244},{24,56},{28,252},{... | collective-permute-start | bytes 1032200 | tf_op jit(solution)/shard_map/ppermute | solution.py:58
  109.2 7.9 %collective-permute-start.15 = (f32[3,3,2,3584]{3,2,1,0:T(2,128)S(1)}, f32[3,3,2,3584]{3,2,1,0:T(2,128)S(1)}, u32[]{:S(2)}, u32[]{:S(2)}) collective-permute-start(f32[3,3,2,3584]{3,2,1,0:T(2,128)S(1)} %constant_dynamic-slice_fusion), channel_id=1, source_target_pairs={{0,4},{4,0},{8,12},{12,8},{16,20},{20,16},{24,28},{28,24},{32,36},... | collective-permute-start | bytes 774152 | tf_op jit(solution)/shard_map/ppermute | solution.py:58
  117.2 2.6 %collective-permute-start.22 = (bf16[3,4,8,3584]{3,2,1,0:T(8,128)(2,1)S(1)}, bf16[3,4,8,3584]{3,2,1,0:T(8,128)(2,1)S(1)}, u32[]{:S(2)}, u32[]{:S(2)}) collective-permute-start(bf16[3,4,8,3584]{3,2,1,0:T(8,128)(2,1)S(1)} %pad_maximum_fusion), channel_id=1, source_target_pairs={{0,32},{4,228},{8,40},{12,236},{16,48},{20,244},{24,56},{28,252},{... | collective-permute-start | bytes 2064392 | tf_op jit(solution)/shard_map/ppermute | solution.py:58
  120.8 0.8 collective-permute-start.25
  123.1 0.9 fusion.15
  124.0 4.2 %collective-permute-done.22 = bf16[3,4,8,3584]{3,2,1,0:T(8,128)(2,1)S(1)} collective-permute-done((bf16[3,4,8,3584]{3,2,1,0:T(8,128)(2,1)S(1)}, bf16[3,4,8,3584]{3,2,1,0:T(8,128)(2,1)S(1)}, u32[]{:S(2)}, u32[]{:S(2)}) %collective-permute-start.22) | collective-permute-done | bytes 688160 | tf_op jit(solution)/shard_map/ppermute | solution.py:58
  128.3 2.2 %collective-permute-start.26 = (bf16[3,4,8,3584]{3,2,1,0:T(8,128)(2,1)S(1)}, bf16[3,4,8,3584]{3,2,1,0:T(8,128)(2,1)S(1)}, u32[]{:S(2)}, u32[]{:S(2)}) collective-permute-start(bf16[3,4,8,3584]{3,2,1,0:T(8,128)(2,1)S(1)} %collective-permute-done.22), channel_id=1, source_target_pairs={{0,4},{4,0},{8,12},{12,8},{16,20},{20,16},{24,28},{28,24},{32,36},... | collective-permute-start | bytes 2064392 | tf_op jit(solution)/shard_map/ppermute | solution.py:58
  130.5 1.2 collective-permute-done.23
  132.3 1.6 %collective-permute-done.27 = bf16[3,8,8,1792]{3,2,1,0:T(8,128)(2,1)S(1)} collective-permute-done((bf16[3,8,8,1792]{3,2,1,0:T(8,128)(2,1)S(1)}, bf16[3,8,8,1792]{3,2,1,0:T(8,128)(2,1)S(1)}, u32[]{:S(2)}, u32[]{:S(2)}) %collective-permute-start.27) | collective-permute-done | bytes 688160 | tf_op jit(solution)/shard_map/ppermute | solution.py:58
  134.0 2.4 %copy-done = bf16[3,4,2,2,8,7168]{5,4,3,2,1,0:T(8,128)(2,1)} copy-done((bf16[3,4,2,2,8,7168]{5,4,3,2,1,0:T(8,128)(2,1)}, bf16[3,4,2,2,8,7168]{5,4,3,2,1,0:T(8,128)(2,1)S(1)}, u32[]{:S(2)}) %copy-start) | copy-done | bytes 5505048
  (89 shorter events, 10.0 us)
Async XLA Ops:
  2.0 0.9 copy-start.2
  2.8 24.5 %collective-permute-start = (f32[3,3,2,3584]{3,2,1,0:T(2,128)S(1)}, f32[3,3,2,3584]{3,2,1,0:T(2,128)}, u32[]{:S(2)}, u32[]{:S(2)}) collective-permute-start(f32[3,3,2,3584]{3,2,1,0:T(2,128)S(1)} %constant_dynamic-slice_fusion.6), channel_id=1, source_target_pairs={{0,4},{4,0},{8,12},{12,8},{16,20},{20,16},{24,28},{28,24},{32,36},... | collective-permute-start | bytes 774152 | tf_op jit(solution)/shard_map/ppermute | solution.py:58
  6.1 4.2 %copy-start.4 = (s32[1,3]{1,0:T(1,128)S(1)}, s32[1,3]{1,0:T(1,128)}, u32[]{:S(2)}) copy-start(s32[1,3]{1,0:T(1,128)} %param.8) | copy-start | bytes 40
  9.6 28.8 %collective-permute-start.3 = (f32[3,8,8,3584]{3,2,1,0:T(8,128)}, f32[3,8,8,3584]{3,2,1,0:T(8,128)}, u32[]{:S(2)}, u32[]{:S(2)}) collective-permute-start(f32[3,8,8,3584]{3,2,1,0:T(8,128)} %dynamic-slice_bitcast_fusion.1), channel_id=1, source_target_pairs={{0,4},{4,0},{8,12},{12,8},{16,20},{20,16},{24,28},{28,24},{32,36},... | collective-permute-start | bytes 8257544 | tf_op jit(solution)/shard_map/ppermute | solution.py:58
  11.0 21.1 %all-to-all-start = ((s32[64,1,4]{2,1,0:T(1,128)}), s32[64,1,4]{2,1,0:T(1,128)S(1)}, u32[]{:S(2)}, u32[]{:S(2)}) async-start(s32[64,1,4]{2,1,0:T(1,128)} %broadcast_in_dim_broadcast_in_dim.2), calls=%async_computation | async-start | bytes 65536 | tf_op jit(solution)/shard_map/all_to_all | solution.py:191
  24.8 19.5 %collective-permute-start.6 = (f32[3,8,8,3584]{3,2,1,0:T(8,128)}, f32[3,8,8,3584]{3,2,1,0:T(8,128)}, u32[]{:S(2)}, u32[]{:S(2)}) collective-permute-start(f32[3,8,8,3584]{3,2,1,0:T(8,128)} %dynamic-slice_bitcast_fusion), channel_id=1, source_target_pairs={{0,4},{4,0},{8,12},{12,8},{16,20},{20,16},{24,28},{28,24},{32,36},... | collective-permute-start | bytes 8257544 | tf_op jit(solution)/shard_map/ppermute | solution.py:58
  25.3 2.0 %copy-start.5 = (f32[3]{0:T(128)S(1)}, f32[3]{0:T(128)}, u32[]{:S(2)}) copy-start(f32[3]{0:T(128)} %param.10) | copy-start | bytes 40
  28.6 3.5 %copy-start.1 = (f32[3,3,2,3584]{3,2,1,0:T(2,128)}, f32[3,3,2,3584]{3,2,1,0:T(2,128)S(1)}, u32[]{:S(2)}) copy-start(f32[3,3,2,3584]{3,2,1,0:T(2,128)S(1)} %get-tuple-element.33) | copy-start | bytes 774148
  29.5 6.7 %collective-permute-start.1 = (f32[3,3,4,1792]{3,2,1,0:T(4,128)}, f32[3,3,4,1792]{3,2,1,0:T(4,128)}, u32[]{:S(2)}, u32[]{:S(2)}) collective-permute-start(f32[3,3,4,1792]{3,2,1,0:T(4,128)} %fusion.12), channel_id=1, source_target_pairs={{0,8},{4,28},{8,0},{12,20},{16,24},{20,12},{24,16},{28,4},{32,40},... | collective-permute-start | bytes 774152 | tf_op jit(solution)/shard_map/ppermute | solution.py:58
  33.5 4.9 %copy-start.3 = (f32[3584]{0:T(1024)S(1)}, f32[3584]{0:T(1024)}, u32[]{:S(2)}) copy-start(f32[3584]{0:T(1024)} %reduce) | copy-start | bytes 43012
  38.0 30.2 %collective-permute-start.2 = (f32[3,3,8,896]{3,2,1,0:T(8,128)}, f32[3,3,8,896]{3,2,1,0:T(8,128)S(1)}, u32[]{:S(2)}, u32[]{:S(2)}) collective-permute-start(f32[3,3,8,896]{3,2,1,0:T(8,128)} %pad_maximum_fusion.5), channel_id=1, source_target_pairs={{0,24},{4,12},{8,16},{12,4},{16,8},{20,28},{24,0},{28,20},{32,56},... | collective-permute-start | bytes 774152 | tf_op jit(solution)/shard_map/ppermute | solution.py:58
  40.0 11.1 %collective-permute-start.4 = (f16[3,4,8,3584]{3,2,1,0:T(8,128)(2,1)S(1)}, f16[3,4,8,3584]{3,2,1,0:T(8,128)(2,1)S(1)}, u32[]{:S(2)}, u32[]{:S(2)}) collective-permute-start(f16[3,4,8,3584]{3,2,1,0:T(8,128)(2,1)S(1)} %fusion.5), channel_id=1, source_target_pairs={{0,32},{4,228},{8,40},{12,236},{16,48},{20,244},{24,56},{28,252},{... | collective-permute-start | bytes 2064392 | tf_op jit(solution)/shard_map/ppermute | solution.py:58
  48.7 11.1 %collective-permute-start.7 = (f16[3,8,8,1792]{3,2,1,0:T(8,128)(2,1)S(1)}, f16[3,8,8,1792]{3,2,1,0:T(8,128)(2,1)S(1)}, u32[]{:S(2)}, u32[]{:S(2)}) collective-permute-start(f16[3,8,8,1792]{3,2,1,0:T(8,128)(2,1)S(1)} %fusion.1), channel_id=1, source_target_pairs={{0,8},{4,28},{8,0},{12,20},{16,24},{20,12},{24,16},{28,4},{32,40},... | collective-permute-start | bytes 2064392 | tf_op jit(solution)/shard_map/ppermute | solution.py:58
  51.3 12.2 %collective-permute-start.5 = (f16[3,4,8,1792]{3,2,1,0:T(8,128)(2,1)S(1)}, f16[3,4,8,1792]{3,2,1,0:T(8,128)(2,1)S(1)}, u32[]{:S(2)}, u32[]{:S(2)}) collective-permute-start(f16[3,4,8,1792]{3,2,1,0:T(8,128)(2,1)S(1)} %dynamic-slice_convert_fusion.1), channel_id=1, source_target_pairs={{0,8},{4,28},{8,0},{12,20},{16,24},{20,12},{24,16},{28,4},{32,40},... | collective-permute-start | bytes 1032200 | tf_op jit(solution)/shard_map/ppermute | solution.py:58
  60.0 7.4 %collective-permute-start.8 = (f16[3,4,8,1792]{3,2,1,0:T(8,128)(2,1)S(1)}, f16[3,4,8,1792]{3,2,1,0:T(8,128)(2,1)S(1)}, u32[]{:S(2)}, u32[]{:S(2)}) collective-permute-start(f16[3,4,8,1792]{3,2,1,0:T(8,128)(2,1)S(1)} %fusion.10), channel_id=1, source_target_pairs={{0,32},{4,228},{8,40},{12,236},{16,48},{20,244},{24,56},{28,252},{... | collective-permute-start | bytes 1032200 | tf_op jit(solution)/shard_map/ppermute | solution.py:58
  67.5 6.5 %collective-permute-start.9 = (f16[3,4,16,896]{3,2,1,0:T(8,128)(2,1)S(1)}, f16[3,4,16,896]{3,2,1,0:T(8,128)(2,1)S(1)}, u32[]{:S(2)}, u32[]{:S(2)}) collective-permute-start(f16[3,4,16,896]{3,2,1,0:T(8,128)(2,1)S(1)} %fusion.7), channel_id=1, source_target_pairs={{0,24},{4,12},{8,16},{12,4},{16,8},{20,28},{24,0},{28,20},{32,56},... | collective-permute-start | bytes 1032200 | tf_op jit(solution)/shard_map/ppermute | solution.py:58
  74.1 5.0 %collective-permute-start.12 = (f16[3,1,16,896]{3,2,1,0:T(8,128)(2,1)S(1)}, f16[3,1,16,896]{3,2,1,0:T(8,128)(2,1)S(1)}, u32[]{:S(2)}, u32[]{:S(2)}) collective-permute-start(f16[3,1,16,896]{3,2,1,0:T(8,128)(2,1)S(1)} %get-tuple-element.43), channel_id=1, source_target_pairs={{0,192},{4,196},{8,200},{12,204},{16,208},{20,212},{24,216},{28,22... | collective-permute-start | bytes 258056 | tf_op jit(solution)/shard_map/ppermute | solution.py:58
  75.0 5.4 %collective-permute-start.11 = (f16[3,1,16,896]{3,2,1,0:T(8,128)(2,1)S(1)}, f16[3,1,16,896]{3,2,1,0:T(8,128)(2,1)S(1)}, u32[]{:S(2)}, u32[]{:S(2)}) collective-permute-start(f16[3,1,16,896]{3,2,1,0:T(8,128)(2,1)S(1)} %get-tuple-element.44), channel_id=1, source_target_pairs={{0,64},{4,68},{8,72},{12,76},{16,80},{20,84},{24,88},{28,92},{32,9... | collective-permute-start | bytes 258056 | tf_op jit(solution)/shard_map/ppermute | solution.py:58
  76.6 8.8 %collective-permute-start.10 = (f16[3,1,16,896]{3,2,1,0:T(8,128)(2,1)S(1)}, f16[3,1,16,896]{3,2,1,0:T(8,128)(2,1)S(1)}, u32[]{:S(2)}, u32[]{:S(2)}) collective-permute-start(f16[3,1,16,896]{3,2,1,0:T(8,128)(2,1)S(1)} %get-tuple-element.42), channel_id=1, source_target_pairs={{0,128},{4,132},{8,136},{12,140},{16,144},{20,148},{24,152},{28,15... | collective-permute-start | bytes 258056 | tf_op jit(solution)/shard_map/ppermute | solution.py:58
  85.6 8.2 %collective-permute-start.16 = (bf16[3,1,16,896]{3,2,1,0:T(8,128)(2,1)S(1)}, bf16[3,1,16,896]{3,2,1,0:T(8,128)(2,1)S(1)}, u32[]{:S(2)}, u32[]{:S(2)}) collective-permute-start(bf16[3,1,16,896]{3,2,1,0:T(8,128)(2,1)S(1)} %get-tuple-element.25), channel_id=1, source_target_pairs={{0,128},{4,132},{8,136},{12,140},{16,144},{20,148},{24,152},{28,15... | collective-permute-start | bytes 258056 | tf_op jit(solution)/shard_map/ppermute | solution.py:58
  86.7 7.1 %collective-permute-start.17 = (bf16[3,1,16,896]{3,2,1,0:T(8,128)(2,1)S(1)}, bf16[3,1,16,896]{3,2,1,0:T(8,128)(2,1)S(1)}, u32[]{:S(2)}, u32[]{:S(2)}) collective-permute-start(bf16[3,1,16,896]{3,2,1,0:T(8,128)(2,1)S(1)} %get-tuple-element.25), channel_id=1, source_target_pairs={{0,64},{4,68},{8,72},{12,76},{16,80},{20,84},{24,88},{28,92},{32,9... | collective-permute-start | bytes 258056 | tf_op jit(solution)/shard_map/ppermute | solution.py:58
  89.3 5.7 %collective-permute-start.18 = (bf16[3,1,16,896]{3,2,1,0:T(8,128)(2,1)S(1)}, bf16[3,1,16,896]{3,2,1,0:T(8,128)(2,1)S(1)}, u32[]{:S(2)}, u32[]{:S(2)}) collective-permute-start(bf16[3,1,16,896]{3,2,1,0:T(8,128)(2,1)S(1)} %get-tuple-element.25), channel_id=1, source_target_pairs={{0,192},{4,196},{8,200},{12,204},{16,208},{20,212},{24,216},{28,22... | collective-permute-start | bytes 258056 | tf_op jit(solution)/shard_map/ppermute | solution.py:58
  90.8 7.0 %collective-permute-start.13 = (f32[3,3,8,896]{3,2,1,0:T(8,128)S(1)}, f32[3,3,8,896]{3,2,1,0:T(8,128)S(1)}, u32[]{:S(2)}, u32[]{:S(2)}) collective-permute-start(f32[3,3,8,896]{3,2,1,0:T(8,128)S(1)} %pad_maximum_fusion.6), channel_id=1, source_target_pairs={{0,8},{4,28},{8,0},{12,20},{16,24},{20,12},{24,16},{28,4},{32,40},... | collective-permute-start | bytes 774152 | tf_op jit(solution)/shard_map/ppermute | solution.py:58
  95.0 6.2 %collective-permute-start.19 = (bf16[3,4,16,896]{3,2,1,0:T(8,128)(2,1)S(1)}, bf16[3,4,16,896]{3,2,1,0:T(8,128)(2,1)S(1)}, u32[]{:S(2)}, u32[]{:S(2)}) collective-permute-start(bf16[3,4,16,896]{3,2,1,0:T(8,128)(2,1)S(1)} %constant_dynamic-update-slice_fusion.2), channel_id=1, source_target_pairs={{0,24},{4,12},{8,16},{12,4},{16,8},{20,28},{24,0},{28,20},{32,56},... | collective-permute-start | bytes 1032200 | tf_op jit(solution)/shard_map/ppermute | solution.py:58
  97.9 11.0 %collective-permute-start.14 = (f32[3,3,8,896]{3,2,1,0:T(8,128)S(1)}, f32[3,3,8,896]{3,2,1,0:T(8,128)S(1)}, u32[]{:S(2)}, u32[]{:S(2)}) collective-permute-start(f32[3,3,8,896]{3,2,1,0:T(8,128)S(1)} %pad_maximum_fusion.7), channel_id=1, source_target_pairs={{0,24},{4,12},{8,16},{12,4},{16,8},{20,28},{24,0},{28,20},{32,56},... | collective-permute-start | bytes 774152 | tf_op jit(solution)/shard_map/ppermute | solution.py:58
  101.4 15.7 %collective-permute-start.20 = (bf16[3,4,8,1792]{3,2,1,0:T(8,128)(2,1)S(1)}, bf16[3,4,8,1792]{3,2,1,0:T(8,128)(2,1)S(1)}, u32[]{:S(2)}, u32[]{:S(2)}) collective-permute-start(bf16[3,4,8,1792]{3,2,1,0:T(8,128)(2,1)S(1)} %get-tuple-element.37), channel_id=1, source_target_pairs={{0,8},{4,28},{8,0},{12,20},{16,24},{20,12},{24,16},{28,4},{32,40},... | collective-permute-start | bytes 1032200 | tf_op jit(solution)/shard_map/ppermute | solution.py:58
  107.2 13.4 %collective-permute-start.21 = (bf16[3,4,8,1792]{3,2,1,0:T(8,128)(2,1)S(1)}, bf16[3,4,8,1792]{3,2,1,0:T(8,128)(2,1)S(1)}, u32[]{:S(2)}, u32[]{:S(2)}) collective-permute-start(bf16[3,4,8,1792]{3,2,1,0:T(8,128)(2,1)S(1)} %get-tuple-element.36), channel_id=1, source_target_pairs={{0,32},{4,228},{8,40},{12,236},{16,48},{20,244},{24,56},{28,252},{... | collective-permute-start | bytes 1032200 | tf_op jit(solution)/shard_map/ppermute | solution.py:58
  109.2 13.7 %collective-permute-start.15 = (f32[3,3,2,3584]{3,2,1,0:T(2,128)S(1)}, f32[3,3,2,3584]{3,2,1,0:T(2,128)S(1)}, u32[]{:S(2)}, u32[]{:S(2)}) collective-permute-start(f32[3,3,2,3584]{3,2,1,0:T(2,128)S(1)} %constant_dynamic-slice_fusion), channel_id=1, source_target_pairs={{0,4},{4,0},{8,12},{12,8},{16,20},{20,16},{24,28},{28,24},{32,36},... | collective-permute-start | bytes 774152 | tf_op jit(solution)/shard_map/ppermute | solution.py:58
  117.2 11.1 %collective-permute-start.22 = (bf16[3,4,8,3584]{3,2,1,0:T(8,128)(2,1)S(1)}, bf16[3,4,8,3584]{3,2,1,0:T(8,128)(2,1)S(1)}, u32[]{:S(2)}, u32[]{:S(2)}) collective-permute-start(bf16[3,4,8,3584]{3,2,1,0:T(8,128)(2,1)S(1)} %pad_maximum_fusion), channel_id=1, source_target_pairs={{0,32},{4,228},{8,40},{12,236},{16,48},{20,244},{24,56},{28,252},{... | collective-permute-start | bytes 2064392 | tf_op jit(solution)/shard_map/ppermute | solution.py:58
  119.8 12.0 %collective-permute-start.24 = (bf16[3,4,8,3584]{3,2,1,0:T(8,128)(2,1)S(1)}, bf16[3,4,8,3584]{3,2,1,0:T(8,128)(2,1)S(1)}, u32[]{:S(2)}, u32[]{:S(2)}) collective-permute-start(bf16[3,4,8,3584]{3,2,1,0:T(8,128)(2,1)S(1)} %pad_maximum_fusion), channel_id=1, source_target_pairs={{0,4},{4,0},{8,12},{12,8},{16,20},{20,16},{24,28},{28,24},{32,36},... | collective-permute-start | bytes 2064392 | tf_op jit(solution)/shard_map/ppermute | solution.py:58
  120.7 11.1 %collective-permute-start.23 = (bf16[3,8,8,1792]{3,2,1,0:T(8,128)(2,1)S(1)}, bf16[3,8,8,1792]{3,2,1,0:T(8,128)(2,1)S(1)}, u32[]{:S(2)}, u32[]{:S(2)}) collective-permute-start(bf16[3,8,8,1792]{3,2,1,0:T(8,128)(2,1)S(1)} %bitcast.181), channel_id=1, source_target_pairs={{0,8},{4,28},{8,0},{12,20},{16,24},{20,12},{24,16},{28,4},{32,40},... | collective-permute-start | bytes 2064392 | tf_op jit(solution)/shard_map/ppermute | solution.py:58
  120.8 11.1 %collective-permute-start.25 = (bf16[3,8,8,1792]{3,2,1,0:T(8,128)(2,1)S(1)}, bf16[3,8,8,1792]{3,2,1,0:T(8,128)(2,1)S(1)}, u32[]{:S(2)}, u32[]{:S(2)}) collective-permute-start(bf16[3,8,8,1792]{3,2,1,0:T(8,128)(2,1)S(1)} %bitcast.182), channel_id=1, source_target_pairs={{0,4},{4,0},{8,12},{12,8},{16,20},{20,16},{24,28},{28,24},{32,36},... | collective-permute-start | bytes 2064392 | tf_op jit(solution)/shard_map/ppermute | solution.py:58
  128.3 4.0 %collective-permute-start.26 = (bf16[3,4,8,3584]{3,2,1,0:T(8,128)(2,1)S(1)}, bf16[3,4,8,3584]{3,2,1,0:T(8,128)(2,1)S(1)}, u32[]{:S(2)}, u32[]{:S(2)}) collective-permute-start(bf16[3,4,8,3584]{3,2,1,0:T(8,128)(2,1)S(1)} %collective-permute-done.22), channel_id=1, source_target_pairs={{0,4},{4,0},{8,12},{12,8},{16,20},{20,16},{24,28},{28,24},{32,36},... | collective-permute-start | bytes 2064392 | tf_op jit(solution)/shard_map/ppermute | solution.py:58
  131.7 2.1 %collective-permute-start.27 = (bf16[3,8,8,1792]{3,2,1,0:T(8,128)(2,1)S(1)}, bf16[3,8,8,1792]{3,2,1,0:T(8,128)(2,1)S(1)}, u32[]{:S(2)}, u32[]{:S(2)}) collective-permute-start(bf16[3,8,8,1792]{3,2,1,0:T(8,128)(2,1)S(1)} %collective-permute-done.23), channel_id=1, source_target_pairs={{0,4},{4,0},{8,12},{12,8},{16,20},{20,16},{24,28},{28,24},{32,36},... | collective-permute-start | bytes 2064392 | tf_op jit(solution)/shard_map/ppermute | solution.py:58
  134.0 2.4 %copy-start = (bf16[3,4,2,2,8,7168]{5,4,3,2,1,0:T(8,128)(2,1)}, bf16[3,4,2,2,8,7168]{5,4,3,2,1,0:T(8,128)(2,1)S(1)}, u32[]{:S(2)}) copy-start(bf16[3,4,2,2,8,7168]{5,4,3,2,1,0:T(8,128)(2,1)S(1)} %constant_dynamic-update-slice_fusion.6) | copy-start | bytes 16515076

commit v3 on v2

--- a/solution.py
+++ b/solution.py
@@ -94,7 +94,8 @@
     return pick_z(value, odd) + got
 
 
-FAR = (2, 1, 3)
+FAR = (1, 3, 2)
+BACK = (2, 1, 3)
 
 
 def sum_quad(value, place):
@@ -104,9 +105,9 @@
 
 def gather_quad(value, place):
     mats, _, *rest = value.shape
-    got = [trade(value, z_ahead, k) for k in FAR]
+    got = [trade(value, z_ahead, k) for k in BACK]
     whole = jnp.zeros((mats, 4, *rest), value.dtype)
-    for k, piece in zip((0, *FAR), (value, *got)):
+    for k, piece in zip((0, *BACK), (value, *got)):
         whole = lax.dynamic_update_slice_in_dim(whole, piece, (place - k) % 4, 1)
     return whole
 
@@ -179,6 +180,44 @@
     )(places, notes, weight)
 
 
+def tiles_kernel(at_ref, grad_ref, first_ref, second_ref, held, arrived, left):
+    at = pl.multiple_of(at_ref[0], 128)
+    outs = (first_ref, second_ref)
+    mats, width = grad_ref.shape[0], first_ref.shape[3]
+    places = [(t, m) for t in range(2) for m in range(mats)]
+    ins = [
+        pltpu.make_async_copy(grad_ref.at[m, :, t, :, pl.ds(at, width)], held.at[t, m], arrived.at[t, m])
+        for t, m in places
+    ]
+    backs = [pltpu.make_async_copy(held.at[t, m], outs[t].at[m], left.at[t, m]) for t, m in places]
+    for copy in ins:
+        copy.start()
+    for copy, back in zip(ins, backs):
+        copy.wait()
+        back.start()
+    for back in backs:
+        back.wait()
+
+
+def tiles_of(grad, core, half):
+    mats, blocks, _, rows, _ = grad.shape
+    shape = (mats, blocks, rows, half)
+    return pl.pallas_call(
+        tiles_kernel,
+        out_shape=[jax.ShapeDtypeStruct(shape, grad.dtype)] * 2,
+        in_specs=[pl.BlockSpec(memory_space=pltpu.SMEM), pl.BlockSpec(memory_space=pl.ANY)],
+        out_specs=[pl.BlockSpec(memory_space=pl.ANY)] * 2,
+        scratch_shapes=[
+            pltpu.VMEM((2, *shape), grad.dtype),
+            pltpu.SemaphoreType.DMA((2, mats)),
+            pltpu.SemaphoreType.DMA((2, mats)),
+        ],
+        cost_estimate=pl.CostEstimate(
+            flops=0, bytes_accessed=4 * mats * blocks * rows * half * 4, transcendentals=0
+        ),
+    )((core * half)[None], grad)
+
+
 def local(gradients, token_counts, modality, loss_weight, master, moment_one, moment_two):
     mats, rows, cols = 3, gradients.shape[1], gradients.shape[3]
     half = cols // 2
@@ -196,11 +235,7 @@
         cut = lax.dynamic_slice(grad, (0, 0, t, 0, core * half), (mats, DEEP, 1, 8, half))
         return cut.reshape(mats, DEEP, 8, half)
 
-    give_a = tile(grad, 0, 1 - mine)
-    grad, give_a = lax.optimization_barrier((grad, give_a))
-    give_b = tile(grad, 1, 1 - mine)
-    grad, give_b = lax.optimization_barrier((grad, give_b))
-    own = [tile(grad, t, mine) for t in range(2)]
+    give_a, give_b = tiles_of(grad, 1 - mine, half)
     raw_a = trade(give_a, core_partner)
     raw_b = trade(give_b, core_partner)
     raw = [raw_a, raw_b]
@@ -212,18 +247,23 @@
     chip = 2 * (WIDE * depth + across)
     scales = scale_rows(notes, loss_weight, jnp.stack([chip + mine, chip + 1 - mine]), half)
 
-    def combined(t, cut):
-        wide = cut(own[t])
-        first, second = (scale[:, : wide.shape[3]] for scale in scales)
-        return wide * first + cut(raw[t]) * second
-
-    give_a = combined(0, lambda v: pick_z(v, 1 - odd)).astype(LINK)
-    give_b = combined(1, lambda v: pick(v, 1 - xb[0], 2, 3)).astype(LINK)
+    def combined_a(index):
+        own = pick_z(tile(grad, 0, mine), index)
+        return own * scales[0] + pick_z(raw[0], index) * scales[1]
+
+    def combined_b(index):
+        at = mine * half + index * (half // 2)
+        own = lax.dynamic_slice(grad, (0, 0, 1, 0, at), (mats, DEEP, 1, 8, half // 2))
+        first, second = (scale[:, : half // 2] for scale in scales)
+        return own[:, :, 0] * first + pick(raw[1], index, 2, 3) * second
+
+    give_a = combined_a(1 - odd).astype(LINK)
+    give_b = combined_b(1 - xb[0]).astype(LINK)
     raw_a, give_a = lax.optimization_barrier((raw[0], give_a))
     raw_b, give_b = lax.optimization_barrier((raw[1], give_b))
     raw = [raw_a, raw_b]
-    part_a = lax.optimization_barrier(combined(0, lambda v: pick_z(v, odd)))
-    part_b = lax.optimization_barrier(combined(1, lambda v: pick(v, xb[0], 2, 3)))
+    part_a = lax.optimization_barrier(combined_a(odd))
+    part_b = lax.optimization_barrier(combined_b(xb[0]))
     got_a = send(give_a, z_partner, 0)
     got_b = send(give_b, x_partner, 0)
     part_a, part_b = part_a + got_a, part_b + got_b
@@ -239,13 +279,13 @@
     state = rows_in_order(groups, across, mine)
 
     summed = sum_quad(part, place)[:, 0] * (1.0 / RAISE)
-    new = adam_update(summed, state[1], state[2], state[0])
-    lean = new[0].astype(jnp.bfloat16)[:, None]
+    weights_new, _, _ = adam_update(summed, state[1], state[2], state[0])
+    lean = weights_new.astype(jnp.bfloat16)[:, None]
 
     lean = gather_quad(lean, place)
     lean = gather_x(lean, xb, 1)
+    lean_b = gather_z(lean[:, :, 8:], odd)
     lean_a = gather_x(lean[:, :, :8], xb, 0)
-    lean_b = gather_z(lean[:, :, 8:], odd)
     got_a, got_b = trade(lean_a, z_partner), trade(lean_b, x_partner, 0)
     whole = jnp.zeros((mats, DEEP // 2, 2, 2, 8, cols), jnp.bfloat16)
     for core in (mine, 1 - mine):
@@ -263,9 +303,10 @@
             whole = lax.dynamic_update_slice(whole, tile_b, (0, 0, 0, 1, 0, at))
     whole = whole.reshape(mats, rows, cols)
 
-    left = join_columns(jnp.stack(new), across, mine, xb)
-    back = both(pick(left, mine, 2, 2), trade(pick(left, 1 - mine, 2, 2), core_partner), mine, 3)
-    outs = [jnp.transpose(back[i], (1, 0, 2)) for i in range(3)]
+    left = join_columns(summed[None], across, mine, xb)
+    back = both(pick(left, mine, 2, 2), trade(pick(left, 1 - mine, 2, 2), core_partner), mine, 3)[0]
+    turned = [jnp.transpose(a, (1, 0, 2)) for a in (moment_one, moment_two, master)]
+    outs = [jnp.transpose(a, (1, 0, 2)) for a in adam_update(back, *turned)]
     return (*outs, jnp.transpose(whole, (1, 0, 2)))
 
 

time: 137 us -> 143 us (1.044)
  waiting for transfers between devices: 40.3 us -> 47.9 us
  Pallas kernels: 0.69 us -> 5.48 us
  local copies, waits for them, and re-layouts: 16.1 us -> 11.7 us
  other arithmetic: 16.9 us -> 14.7 us
    ppermute x28, waiting for transfers between devices: 40.3 us -> 47.9 us  [trade(): return lax.ppermute(value, DP, perm)]
    reshape x2 -> x0, local copies, waits for them, and re-layouts: 7.01 us -> none  [tile(): return cut.reshape(mats, DEEP, 8, half)]
    pallas_call x0 -> x1, Pallas kernels: none -> 4.79 us  [tiles_of(): pl.pallas_call(tiles_kernel, out_shape=[jax.ShapeDtypeStruct(shape, grad....]
    unnamed x12 -> x18, local copies, waits for them, and re-layouts: 3.32 us -> 3.3 us
  transfers between devices with their start and end apart: 29 -> 29, of which waited for: 15 -> 16; matrix products, arithmetic and copies ran while one was open for 21% -> 15% of each run, Pallas kernels for 1% -> 0%
where the time goes in v3:
time: 143 us
  starting transfers between devices  61 us (43%)
  waiting for transfers between devices  47.9 us (33%)
  other arithmetic  14.7 us (10%)
  local copies, waits for them, and re-layouts  11.7 us (8%)
  Pallas kernels  5.48 us (4%)
  between operations  1.84 us (1%)
    ppermute x28, starting transfers between devices, trade(): return lax.ppermute(value, DP, perm)  51.1 us
    ppermute x28, waiting for transfers between devices, trade(): return lax.ppermute(value, DP, perm)  47.9 us
    all_to_all x1, starting transfers between devices, local(): notes = lax.all_to_all(notes, DP, 0, 0, tiled=True)  9.89 us
    pallas_call x1, Pallas kernels, tiles_of(): pl.pallas_call(tiles_kernel, out_shape=[jax.ShapeDtypeStruct(shape, grad....  4.79 us
    unnamed x18, local copies, waits for them, and re-layouts  3.3 us
  transfers between devices with their start and end apart: 29, of which 16 were waited for; matrix products, arithmetic and copies ran while one was open for 15% of the time, Pallas kernels for 0%

profile of v3, /device:TPU:1, one launch (start us, length us, event | category | flops | bytes accessed | tf_op | source)
XLA Modules:
  0.0 142.7 jit_solution(3095655406095367675)
XLA Ops:
  0.7 4.8 %shard_map.103 = (f32[3,8,8,3584]{3,2,1,0:T(8,128)}, f32[3,8,8,3584]{3,2,1,0:T(8,128)}) custom-call(s32[1]{0:T(128)} %bitcast.12.at_ref, f32[3,8,2,8,7168]{4,3,2,1,0:T(8,128)} %bitcast.205), custom_call_target="tpu_custom_call" | custom-call | bytes 11010048 | tf_op jit(solution)/shard_map/pallas_call | solution.py:205
  5.5 3.3 %collective-permute-start = (f32[3,8,8,3584]{3,2,1,0:T(8,128)}, f32[3,8,8,3584]{3,2,1,0:T(8,128)}, u32[]{:S(2)}, u32[]{:S(2)}) collective-permute-start(f32[3,8,8,3584]{3,2,1,0:T(8,128)} %get-tuple-element.13), channel_id=1, source_target_pairs={{0,4},{4,0},{8,12},{12,8},{16,20},{20,16},{24,28},{28,24},{32,36},... | collective-permute-start | bytes 8257544 | tf_op jit(solution)/shard_map/ppermute | solution.py:58
  10.1 9.9 %all-to-all-start = ((s32[64,1,4]{2,1,0:T(1,128)}), s32[64,1,4]{2,1,0:T(1,128)S(1)}, u32[]{:S(2)}, u32[]{:S(2)}) async-start(s32[64,1,4]{2,1,0:T(1,128)} %broadcast_in_dim_broadcast_in_dim.2), calls=%async_computation | async-start | bytes 65536 | tf_op jit(solution)/shard_map/all_to_all | solution.py:230
  20.9 0.8 copy-done.1
  21.9 2.0 %constant_dynamic-slice_fusion.3 = f32[3,8,1,8,3584]{4,3,2,1,0:T(8,128)S(1)} fusion(f32[3,8,2,8,7168]{4,3,2,1,0:T(8,128)} %bitcast.206, s32[]{:T(128)S(6)} %select_n.246), kind=kLoop, calls=%fused_computation.114 | loop fusion | bytes 5505028 | tf_op jit(solution)/shard_map/dynamic_slice | solution.py:235
  23.9 2.1 %collective-permute-done.13 = f32[3,3,2,3584]{3,2,1,0:T(2,128)} collective-permute-done((f32[3,3,2,3584]{3,2,1,0:T(2,128)S(1)}, f32[3,3,2,3584]{3,2,1,0:T(2,128)}, u32[]{:S(2)}, u32[]{:S(2)}) %collective-permute-start.13) | collective-permute-done | bytes 258080 | tf_op jit(solution)/shard_map/ppermute | solution.py:58
  26.0 1.3 broadcast_select_fusion.4
  27.3 0.9 fusion.12
  28.2 2.5 %collective-permute-start.14 = (f32[3,3,4,1792]{3,2,1,0:T(4,128)}, f32[3,3,4,1792]{3,2,1,0:T(4,128)}, u32[]{:S(2)}, u32[]{:S(2)}) collective-permute-start(f32[3,3,4,1792]{3,2,1,0:T(4,128)} %fusion.12), channel_id=1, source_target_pairs={{0,8},{4,28},{8,0},{12,20},{16,24},{20,12},{24,16},{28,4},{32,40},... | collective-permute-start | bytes 774152 | tf_op jit(solution)/shard_map/ppermute | solution.py:58
  31.6 0.9 broadcast_in_dim.49
  32.5 1.0 fusion.29
  33.5 1.4 collective-permute-done.14
  34.9 1.7 %constant_dynamic-slice_fusion = (f32[3,3,4,896]{3,2,1,0:T(4,128)S(1)}, f32[3,3,16,896]{3,2,1,0:T(8,128)}) fusion(f32[3,3,4,1792]{3,2,1,0:T(4,128)} %collective-permute-done.14, s32[]{:T(128)S(6)} %select_n.257, f32[3,3,16,896]{3,2,1,0:T(8,128)} %get-tuple-element.36, s32[]{:T(128)S(6)} %select_n.268, s32[]{:T(128)S(6)} %select_n.256), kind=kLoop, calls=%fused_computation.110 | loop fusion | bytes 516108 | tf_op jit(solution)/shard_map/dynamic_slice | solution.py:68
  37.1 1.6 %fusion.5 = f16[3,4,8,3584]{3,2,1,0:T(8,128)(2,1)S(1)} fusion(f32[3,4,2,8,3584]{4,3,2,1,0:T(8,128)} %bitcast.16, s32[]{:T(128)S(6)} %select_n.249, f32[3,4,2,8,3584]{4,3,2,1,0:T(8,128)S(1)} %bitcast.209, f32[3584]{0:T(1024)S(1)} %reduce.1, f32[3584]{0:T(1024)S(1)} %reduce), kind=kLoop, calls=%fused_computation.13 | loop fusion | flops 1376256 | bytes 3469316 | tf_op jit(solution)/shard_map/convert_element_type | solution.py:260
  38.7 2.8 %collective-permute-start.1 = (f16[3,4,8,3584]{3,2,1,0:T(8,128)(2,1)S(1)}, f16[3,4,8,3584]{3,2,1,0:T(8,128)(2,1)S(1)}, u32[]{:S(2)}, u32[]{:S(2)}) collective-permute-start(f16[3,4,8,3584]{3,2,1,0:T(8,128)(2,1)S(1)} %fusion.5), channel_id=1, source_target_pairs={{0,32},{4,228},{8,40},{12,236},{16,48},{20,244},{24,56},{28,252},{... | collective-permute-start | bytes 2064392 | tf_op jit(solution)/shard_map/ppermute | solution.py:58
  41.4 1.5 %fusion.3 = f32[3,4,8,3584]{3,2,1,0:T(8,128)S(1)} fusion(f32[3,4,2,8,3584]{4,3,2,1,0:T(8,128)} %bitcast.18, s32[]{:T(128)S(6)} %select_n.248, f32[3,4,2,8,3584]{4,3,2,1,0:T(8,128)S(1)} %bitcast.210, f32[3584]{0:T(1024)S(1)} %reduce.1, f32[3584]{0:T(1024)S(1)} %reduce), kind=kLoop, calls=%fused_computation.10 | loop fusion | flops 1032192 | bytes 4157444 | tf_op jit(solution)/shard_map/add | solution.py:252
  43.0 2.0 %fusion.1 = f16[3,8,8,1792]{3,2,1,0:T(8,128)(2,1)S(1)} fusion(f32[3,8,8,3584]{3,2,1,0:T(8,128)} %collective-permute-done.3, s32[]{:T(128)S(6)} %select_n.253, f32[3,8,2,8,7168]{4,3,2,1,0:T(8,128)} %bitcast.207, s32[]{:T(128)S(6)} %select_n.255, f32[1792]{0:T(1024)S(1)} %get-tuple-element.49, f32[1792]{0:T(1024)S(1)} %get-tuple-element.50), kind=kLoop, calls=%fused_computation.6 | loop fusion | flops 1376256 | bytes 3454984 | tf_op jit(solution)/shard_map/convert_element_type | solution.py:261
  44.9 1.9 %fusion.2 = f32[3,8,8,1792]{3,2,1,0:T(8,128)S(1)} fusion(f32[3,8,8,3584]{3,2,1,0:T(8,128)} %collective-permute-done.3, s32[]{:T(128)S(6)} %select_n.252, f32[3,8,2,8,7168]{4,3,2,1,0:T(8,128)} %bitcast.208, s32[]{:T(128)S(6)} %select_n.254, f32[1792]{0:T(1024)S(1)} %get-tuple-element.49, f32[1792]{0:T(1024)S(1)} %get-tuple-element.50), kind=kLoop, calls=%fused_computation.8 | loop fusion | flops 1032192 | bytes 4143112 | tf_op jit(solution)/shard_map/add | solution.py:258
  46.9 2.3 %collective-permute-start.4 = (f16[3,8,8,1792]{3,2,1,0:T(8,128)(2,1)S(1)}, f16[3,8,8,1792]{3,2,1,0:T(8,128)(2,1)S(1)}, u32[]{:S(2)}, u32[]{:S(2)}) collective-permute-start(f16[3,8,8,1792]{3,2,1,0:T(8,128)(2,1)S(1)} %fusion.1), channel_id=1, source_target_pairs={{0,8},{4,28},{8,0},{12,20},{16,24},{20,12},{24,16},{28,4},{32,40},... | collective-permute-start | bytes 2064392 | tf_op jit(solution)/shard_map/ppermute | solution.py:58
  50.0 2.3 %collective-permute-start.2 = (f16[3,4,8,1792]{3,2,1,0:T(8,128)(2,1)S(1)}, f16[3,4,8,1792]{3,2,1,0:T(8,128)(2,1)S(1)}, u32[]{:S(2)}, u32[]{:S(2)}) collective-permute-start(f16[3,4,8,1792]{3,2,1,0:T(8,128)(2,1)S(1)} %dynamic-slice_convert_fusion), channel_id=1, source_target_pairs={{0,8},{4,28},{8,0},{12,20},{16,24},{20,12},{24,16},{28,4},{32,40},... | collective-permute-start | bytes 1032200 | tf_op jit(solution)/shard_map/ppermute | solution.py:58
  52.2 5.7 %collective-permute-done.4 = f16[3,8,8,1792]{3,2,1,0:T(8,128)(2,1)S(1)} collective-permute-done((f16[3,8,8,1792]{3,2,1,0:T(8,128)(2,1)S(1)}, f16[3,8,8,1792]{3,2,1,0:T(8,128)(2,1)S(1)}, u32[]{:S(2)}, u32[]{:S(2)}) %collective-permute-start.4) | collective-permute-done | bytes 688160 | tf_op jit(solution)/shard_map/ppermute | solution.py:58
  58.3 3.4 %collective-permute-done.2 = f16[3,4,8,1792]{3,2,1,0:T(8,128)(2,1)S(1)} collective-permute-done((f16[3,4,8,1792]{3,2,1,0:T(8,128)(2,1)S(1)}, f16[3,4,8,1792]{3,2,1,0:T(8,128)(2,1)S(1)}, u32[]{:S(2)}, u32[]{:S(2)}) %collective-permute-start.2) | collective-permute-done | bytes 344096 | tf_op jit(solution)/shard_map/ppermute | solution.py:58
  61.7 3.8 %collective-permute-done.5 = f16[3,4,8,1792]{3,2,1,0:T(8,128)(2,1)S(1)} collective-permute-done((f16[3,4,8,1792]{3,2,1,0:T(8,128)(2,1)S(1)}, f16[3,4,8,1792]{3,2,1,0:T(8,128)(2,1)S(1)}, u32[]{:S(2)}, u32[]{:S(2)}) %collective-permute-start.5) | collective-permute-done | bytes 344096 | tf_op jit(solution)/shard_map/ppermute | solution.py:58
  65.7 0.7 collective-permute-start.6
  67.1 5.0 %collective-permute-done.6 = f16[3,4,16,896]{3,2,1,0:T(8,128)(2,1)S(1)} collective-permute-done((f16[3,4,16,896]{3,2,1,0:T(8,128)(2,1)S(1)}, f16[3,4,16,896]{3,2,1,0:T(8,128)(2,1)S(1)}, u32[]{:S(2)}, u32[]{:S(2)}) %collective-permute-start.6) | collective-permute-done | bytes 344096 | tf_op jit(solution)/shard_map/ppermute | solution.py:58
  72.3 2.6 %collective-permute-start.9 = (f16[3,1,16,896]{3,2,1,0:T(8,128)(2,1)S(1)}, f16[3,1,16,896]{3,2,1,0:T(8,128)(2,1)S(1)}, u32[]{:S(2)}, u32[]{:S(2)}) collective-permute-start(f16[3,1,16,896]{3,2,1,0:T(8,128)(2,1)S(1)} %get-tuple-element.33), channel_id=1, source_target_pairs={{0,128},{4,132},{8,136},{12,140},{16,144},{20,148},{24,152},{28,15... | collective-permute-start | bytes 258056 | tf_op jit(solution)/shard_map/ppermute | solution.py:58
  74.8 2.4 %collective-permute-start.7 = (f16[3,1,16,896]{3,2,1,0:T(8,128)(2,1)S(1)}, f16[3,1,16,896]{3,2,1,0:T(8,128)(2,1)S(1)}, u32[]{:S(2)}, u32[]{:S(2)}) collective-permute-start(f16[3,1,16,896]{3,2,1,0:T(8,128)(2,1)S(1)} %get-tuple-element.32), channel_id=1, source_target_pairs={{0,64},{4,68},{8,72},{12,76},{16,80},{20,84},{24,88},{28,92},{32,9... | collective-permute-start | bytes 258056 | tf_op jit(solution)/shard_map/ppermute | solution.py:58
  77.9 2.7 %collective-permute-done.9 = f16[3,1,16,896]{3,2,1,0:T(8,128)(2,1)S(1)} collective-permute-done((f16[3,1,16,896]{3,2,1,0:T(8,128)(2,1)S(1)}, f16[3,1,16,896]{3,2,1,0:T(8,128)(2,1)S(1)}, u32[]{:S(2)}, u32[]{:S(2)}) %collective-permute-start.9) | collective-permute-done | bytes 86048 | tf_op jit(solution)/shard_map/ppermute | solution.py:58
  80.7 1.3 constant_dynamic-update-slice_fusion.5
  82.0 3.5 %collective-permute-start.16 = (bf16[3,1,16,896]{3,2,1,0:T(8,128)(2,1)S(1)}, bf16[3,1,16,896]{3,2,1,0:T(8,128)(2,1)S(1)}, u32[]{:S(2)}, u32[]{:S(2)}) collective-permute-start(bf16[3,1,16,896]{3,2,1,0:T(8,128)(2,1)S(1)} %get-tuple-element.21), channel_id=1, source_target_pairs={{0,128},{4,132},{8,136},{12,140},{16,144},{20,148},{24,152},{28,15... | collective-permute-start | bytes 258056 | tf_op jit(solution)/shard_map/ppermute | solution.py:58
  85.9 3.2 %collective-permute-start.18 = (bf16[3,1,16,896]{3,2,1,0:T(8,128)(2,1)S(1)}, bf16[3,1,16,896]{3,2,1,0:T(8,128)(2,1)S(1)}, u32[]{:S(2)}, u32[]{:S(2)}) collective-permute-start(bf16[3,1,16,896]{3,2,1,0:T(8,128)(2,1)S(1)} %get-tuple-element.21), channel_id=1, source_target_pairs={{0,192},{4,196},{8,200},{12,204},{16,208},{20,212},{24,216},{28,22... | collective-permute-start | bytes 258056 | tf_op jit(solution)/shard_map/ppermute | solution.py:58
  89.2 5.0 %collective-permute-start.10 = (f32[1,3,8,896]{3,2,1,0:T(8,128)S(1)}, f32[1,3,8,896]{3,2,1,0:T(8,128)S(1)}, u32[]{:S(2)}, u32[]{:S(2)}) collective-permute-start(f32[1,3,8,896]{3,2,1,0:T(8,128)S(1)} %pad_maximum_fusion.5), channel_id=1, source_target_pairs={{0,8},{4,28},{8,0},{12,20},{16,24},{20,12},{24,16},{28,4},{32,40},... | collective-permute-start | bytes 258056 | tf_op jit(solution)/shard_map/ppermute | solution.py:58
  94.3 1.8 %collective-permute-done.10 = f32[1,3,8,896]{3,2,1,0:T(8,128)S(1)} collective-permute-done((f32[1,3,8,896]{3,2,1,0:T(8,128)S(1)}, f32[1,3,8,896]{3,2,1,0:T(8,128)S(1)}, u32[]{:S(2)}, u32[]{:S(2)}) %collective-permute-start.10) | collective-permute-done | bytes 86048 | tf_op jit(solution)/shard_map/ppermute | solution.py:58
  96.1 1.5 %collective-permute-start.11 = (f32[1,3,8,896]{3,2,1,0:T(8,128)S(1)}, f32[1,3,8,896]{3,2,1,0:T(8,128)S(1)}, u32[]{:S(2)}, u32[]{:S(2)}) collective-permute-start(f32[1,3,8,896]{3,2,1,0:T(8,128)S(1)} %pad_maximum_fusion.6), channel_id=1, source_target_pairs={{0,24},{4,12},{8,16},{12,4},{16,8},{20,28},{24,0},{28,20},{32,56},... | collective-permute-start | bytes 258056 | tf_op jit(solution)/shard_map/ppermute | solution.py:58
  97.7 2.2 %collective-permute-done.11 = f32[1,3,8,896]{3,2,1,0:T(8,128)S(1)} collective-permute-done((f32[1,3,8,896]{3,2,1,0:T(8,128)S(1)}, f32[1,3,8,896]{3,2,1,0:T(8,128)S(1)}, u32[]{:S(2)}, u32[]{:S(2)}) %collective-permute-start.11) | collective-permute-done | bytes 86048 | tf_op jit(solution)/shard_map/ppermute | solution.py:58
  100.0 8.2 %collective-permute-start.12 = (f32[1,3,2,3584]{3,2,1,0:T(2,128)S(1)}, f32[1,3,2,3584]{3,2,1,0:T(2,128)S(1)}, u32[]{:S(2)}, u32[]{:S(2)}) collective-permute-start(f32[1,3,2,3584]{3,2,1,0:T(2,128)S(1)} %constant_dynamic-slice_fusion.2), channel_id=1, source_target_pairs={{0,4},{4,0},{8,12},{12,8},{16,20},{20,16},{24,28},{28,24},{32,36},... | collective-permute-start | bytes 258056 | tf_op jit(solution)/shard_map/ppermute | solution.py:58
  108.3 0.8 collective-permute-done.12
  109.2 5.5 %collective-permute-done.19 = bf16[3,4,16,896]{3,2,1,0:T(8,128)(2,1)S(1)} collective-permute-done((bf16[3,4,16,896]{3,2,1,0:T(8,128)(2,1)S(1)}, bf16[3,4,16,896]{3,2,1,0:T(8,128)(2,1)S(1)}, u32[]{:S(2)}, u32[]{:S(2)}) %collective-permute-start.19) | collective-permute-done | bytes 344096 | tf_op jit(solution)/shard_map/ppermute | solution.py:58
  114.9 1.3 fusion.33
  116.3 1.2 collective-permute-start.21
  117.5 4.7 %collective-permute-done.20 = bf16[3,4,8,1792]{3,2,1,0:T(8,128)(2,1)S(1)} collective-permute-done((bf16[3,4,8,1792]{3,2,1,0:T(8,128)(2,1)S(1)}, bf16[3,4,8,1792]{3,2,1,0:T(8,128)(2,1)S(1)}, u32[]{:S(2)}, u32[]{:S(2)}) %collective-permute-start.20) | collective-permute-done | bytes 344096 | tf_op jit(solution)/shard_map/ppermute | solution.py:58
  123.0 3.8 %collective-permute-start.24 = (bf16[3,4,8,3584]{3,2,1,0:T(8,128)(2,1)S(1)}, bf16[3,4,8,3584]{3,2,1,0:T(8,128)(2,1)S(1)}, u32[]{:S(2)}, u32[]{:S(2)}) collective-permute-start(bf16[3,4,8,3584]{3,2,1,0:T(8,128)(2,1)S(1)} %pad_maximum_fusion), channel_id=1, source_target_pairs={{0,4},{4,0},{8,12},{12,8},{16,20},{20,16},{24,28},{28,24},{32,36},... | collective-permute-start | bytes 2064392 | tf_op jit(solution)/shard_map/ppermute | solution.py:58
  127.0 1.1 collective-permute-start.25
  129.4 4.0 %collective-permute-done.22 = bf16[3,4,8,3584]{3,2,1,0:T(8,128)(2,1)S(1)} collective-permute-done((bf16[3,4,8,3584]{3,2,1,0:T(8,128)(2,1)S(1)}, bf16[3,4,8,3584]{3,2,1,0:T(8,128)(2,1)S(1)}, u32[]{:S(2)}, u32[]{:S(2)}) %collective-permute-start.22) | collective-permute-done | bytes 688160 | tf_op jit(solution)/shard_map/ppermute | solution.py:58
  133.4 2.3 %collective-permute-start.26 = (bf16[3,4,8,3584]{3,2,1,0:T(8,128)(2,1)S(1)}, bf16[3,4,8,3584]{3,2,1,0:T(8,128)(2,1)S(1)}, u32[]{:S(2)}, u32[]{:S(2)}) collective-permute-start(bf16[3,4,8,3584]{3,2,1,0:T(8,128)(2,1)S(1)} %collective-permute-done.22), channel_id=1, source_target_pairs={{0,4},{4,0},{8,12},{12,8},{16,20},{20,16},{24,28},{28,24},{32,36},... | collective-permute-start | bytes 2064392 | tf_op jit(solution)/shard_map/ppermute | solution.py:58
  135.8 2.2 %collective-permute-done.23 = bf16[3,8,8,1792]{3,2,1,0:T(8,128)(2,1)S(1)} collective-permute-done((bf16[3,8,8,1792]{3,2,1,0:T(8,128)(2,1)S(1)}, bf16[3,8,8,1792]{3,2,1,0:T(8,128)(2,1)S(1)}, u32[]{:S(2)}, u32[]{:S(2)}) %collective-permute-start.23) | collective-permute-done | bytes 688160 | tf_op jit(solution)/shard_map/ppermute | solution.py:58
  138.3 1.8 %collective-permute-done.27 = bf16[3,8,8,1792]{3,2,1,0:T(8,128)(2,1)S(1)} collective-permute-done((bf16[3,8,8,1792]{3,2,1,0:T(8,128)(2,1)S(1)}, bf16[3,8,8,1792]{3,2,1,0:T(8,128)(2,1)S(1)}, u32[]{:S(2)}, u32[]{:S(2)}) %collective-permute-start.27) | collective-permute-done | bytes 688160 | tf_op jit(solution)/shard_map/ppermute | solution.py:58
  140.2 2.4 %copy-done = bf16[3,4,2,2,8,7168]{5,4,3,2,1,0:T(8,128)(2,1)} copy-done((bf16[3,4,2,2,8,7168]{5,4,3,2,1,0:T(8,128)(2,1)}, bf16[3,4,2,2,8,7168]{5,4,3,2,1,0:T(8,128)(2,1)S(1)}, u32[]{:S(2)}) %copy-start) | copy-done | bytes 5505048
  (94 shorter events, 9.7 us)
Async XLA Ops:
  0.6 8.8 %copy-start.7 = (s32[1,3]{1,0:T(1,128)S(1)}, s32[1,3]{1,0:T(1,128)}, u32[]{:S(2)}) copy-start(s32[1,3]{1,0:T(1,128)} %param.8) | copy-start | bytes 40
  0.7 19.9 %copy-start.2 = (f32[2,3,7168]{2,0,1:T(2,128)S(1)}, f32[2,3,7168]{2,0,1:T(2,128)}, u32[]{:S(2)}) copy-start(f32[2,3,7168]{2,0,1:T(2,128)} %param.13) | copy-start | bytes 516100
  0.7 19.9 %copy-start.3 = (f32[2,3,7168]{2,0,1:T(2,128)S(1)}, f32[2,3,7168]{2,0,1:T(2,128)}, u32[]{:S(2)}) copy-start(f32[2,3,7168]{2,0,1:T(2,128)} %param.12) | copy-start | bytes 516100
  0.7 19.9 %copy-start.5 = (f32[2,3,7168]{2,0,1:T(2,128)S(1)}, f32[2,3,7168]{2,0,1:T(2,128)}, u32[]{:S(2)}) copy-start(f32[2,3,7168]{2,0,1:T(2,128)} %param.11) | copy-start | bytes 516100
  5.5 31.6 %collective-permute-start = (f32[3,8,8,3584]{3,2,1,0:T(8,128)}, f32[3,8,8,3584]{3,2,1,0:T(8,128)}, u32[]{:S(2)}, u32[]{:S(2)}) collective-permute-start(f32[3,8,8,3584]{3,2,1,0:T(8,128)} %get-tuple-element.13), channel_id=1, source_target_pairs={{0,4},{4,0},{8,12},{12,8},{16,20},{20,16},{24,28},{28,24},{32,36},... | collective-permute-start | bytes 8257544 | tf_op jit(solution)/shard_map/ppermute | solution.py:58
  10.1 20.6 %all-to-all-start = ((s32[64,1,4]{2,1,0:T(1,128)}), s32[64,1,4]{2,1,0:T(1,128)S(1)}, u32[]{:S(2)}, u32[]{:S(2)}) async-start(s32[64,1,4]{2,1,0:T(1,128)} %broadcast_in_dim_broadcast_in_dim.2), calls=%async_computation | async-start | bytes 65536 | tf_op jit(solution)/shard_map/all_to_all | solution.py:230
  20.0 22.9 %collective-permute-start.3 = (f32[3,8,8,3584]{3,2,1,0:T(8,128)}, f32[3,8,8,3584]{3,2,1,0:T(8,128)}, u32[]{:S(2)}, u32[]{:S(2)}) collective-permute-start(f32[3,8,8,3584]{3,2,1,0:T(8,128)} %get-tuple-element.17), channel_id=1, source_target_pairs={{0,4},{4,0},{8,12},{12,8},{16,20},{20,16},{24,28},{28,24},{32,36},... | collective-permute-start | bytes 8257544 | tf_op jit(solution)/shard_map/ppermute | solution.py:58
  20.9 0.8 copy-start.1
  21.7 4.3 %collective-permute-start.13 = (f32[3,3,2,3584]{3,2,1,0:T(2,128)S(1)}, f32[3,3,2,3584]{3,2,1,0:T(2,128)}, u32[]{:S(2)}, u32[]{:S(2)}) collective-permute-start(f32[3,3,2,3584]{3,2,1,0:T(2,128)S(1)} %constant_dynamic-slice_fusion.1), channel_id=1, source_target_pairs={{0,4},{4,0},{8,12},{12,8},{16,20},{20,16},{24,28},{28,24},{32,36},... | collective-permute-start | bytes 774152 | tf_op jit(solution)/shard_map/ppermute | solution.py:58
  21.9 2.0 %copy-start.8 = (f32[3]{0:T(128)S(1)}, f32[3]{0:T(128)}, u32[]{:S(2)}) copy-start(f32[3]{0:T(128)} %param.10) | copy-start | bytes 40
  28.2 6.7 %collective-permute-start.14 = (f32[3,3,4,1792]{3,2,1,0:T(4,128)}, f32[3,3,4,1792]{3,2,1,0:T(4,128)}, u32[]{:S(2)}, u32[]{:S(2)}) collective-permute-start(f32[3,3,4,1792]{3,2,1,0:T(4,128)} %fusion.12), channel_id=1, source_target_pairs={{0,8},{4,28},{8,0},{12,20},{16,24},{20,12},{24,16},{28,4},{32,40},... | collective-permute-start | bytes 774152 | tf_op jit(solution)/shard_map/ppermute | solution.py:58
  36.6 29.8 %collective-permute-start.15 = (f32[3,3,8,896]{3,2,1,0:T(8,128)S(1)}, f32[3,3,8,896]{3,2,1,0:T(8,128)S(1)}, u32[]{:S(2)}, u32[]{:S(2)}) collective-permute-start(f32[3,3,8,896]{3,2,1,0:T(8,128)S(1)} %pad_maximum_fusion.4), channel_id=1, source_target_pairs={{0,24},{4,12},{8,16},{12,4},{16,8},{20,28},{24,0},{28,20},{32,56},... | collective-permute-start | bytes 774152 | tf_op jit(solution)/shard_map/ppermute | solution.py:58
  38.7 11.1 %collective-permute-start.1 = (f16[3,4,8,3584]{3,2,1,0:T(8,128)(2,1)S(1)}, f16[3,4,8,3584]{3,2,1,0:T(8,128)(2,1)S(1)}, u32[]{:S(2)}, u32[]{:S(2)}) collective-permute-start(f16[3,4,8,3584]{3,2,1,0:T(8,128)(2,1)S(1)} %fusion.5), channel_id=1, source_target_pairs={{0,32},{4,228},{8,40},{12,236},{16,48},{20,244},{24,56},{28,252},{... | collective-permute-start | bytes 2064392 | tf_op jit(solution)/shard_map/ppermute | solution.py:58
  46.9 11.1 %collective-permute-start.4 = (f16[3,8,8,1792]{3,2,1,0:T(8,128)(2,1)S(1)}, f16[3,8,8,1792]{3,2,1,0:T(8,128)(2,1)S(1)}, u32[]{:S(2)}, u32[]{:S(2)}) collective-permute-start(f16[3,8,8,1792]{3,2,1,0:T(8,128)(2,1)S(1)} %fusion.1), channel_id=1, source_target_pairs={{0,8},{4,28},{8,0},{12,20},{16,24},{20,12},{24,16},{28,4},{32,40},... | collective-permute-start | bytes 2064392 | tf_op jit(solution)/shard_map/ppermute | solution.py:58
  50.0 11.7 %collective-permute-start.2 = (f16[3,4,8,1792]{3,2,1,0:T(8,128)(2,1)S(1)}, f16[3,4,8,1792]{3,2,1,0:T(8,128)(2,1)S(1)}, u32[]{:S(2)}, u32[]{:S(2)}) collective-permute-start(f16[3,4,8,1792]{3,2,1,0:T(8,128)(2,1)S(1)} %dynamic-slice_convert_fusion), channel_id=1, source_target_pairs={{0,8},{4,28},{8,0},{12,20},{16,24},{20,12},{24,16},{28,4},{32,40},... | collective-permute-start | bytes 1032200 | tf_op jit(solution)/shard_map/ppermute | solution.py:58
  58.1 7.4 %collective-permute-start.5 = (f16[3,4,8,1792]{3,2,1,0:T(8,128)(2,1)S(1)}, f16[3,4,8,1792]{3,2,1,0:T(8,128)(2,1)S(1)}, u32[]{:S(2)}, u32[]{:S(2)}) collective-permute-start(f16[3,4,8,1792]{3,2,1,0:T(8,128)(2,1)S(1)} %fusion.10), channel_id=1, source_target_pairs={{0,32},{4,228},{8,40},{12,236},{16,48},{20,244},{24,56},{28,252},{... | collective-permute-start | bytes 1032200 | tf_op jit(solution)/shard_map/ppermute | solution.py:58
  65.7 6.5 %collective-permute-start.6 = (f16[3,4,16,896]{3,2,1,0:T(8,128)(2,1)S(1)}, f16[3,4,16,896]{3,2,1,0:T(8,128)(2,1)S(1)}, u32[]{:S(2)}, u32[]{:S(2)}) collective-permute-start(f16[3,4,16,896]{3,2,1,0:T(8,128)(2,1)S(1)} %fusion.7), channel_id=1, source_target_pairs={{0,24},{4,12},{8,16},{12,4},{16,8},{20,28},{24,0},{28,20},{32,56},... | collective-permute-start | bytes 1032200 | tf_op jit(solution)/shard_map/ppermute | solution.py:58
  72.3 8.3 %collective-permute-start.9 = (f16[3,1,16,896]{3,2,1,0:T(8,128)(2,1)S(1)}, f16[3,1,16,896]{3,2,1,0:T(8,128)(2,1)S(1)}, u32[]{:S(2)}, u32[]{:S(2)}) collective-permute-start(f16[3,1,16,896]{3,2,1,0:T(8,128)(2,1)S(1)} %get-tuple-element.33), channel_id=1, source_target_pairs={{0,128},{4,132},{8,136},{12,140},{16,144},{20,148},{24,152},{28,15... | collective-permute-start | bytes 258056 | tf_op jit(solution)/shard_map/ppermute | solution.py:58
  74.8 5.8 %collective-permute-start.8 = (f16[3,1,16,896]{3,2,1,0:T(8,128)(2,1)S(1)}, f16[3,1,16,896]{3,2,1,0:T(8,128)(2,1)S(1)}, u32[]{:S(2)}, u32[]{:S(2)}) collective-permute-start(f16[3,1,16,896]{3,2,1,0:T(8,128)(2,1)S(1)} %get-tuple-element.34), channel_id=1, source_target_pairs={{0,192},{4,196},{8,200},{12,204},{16,208},{20,212},{24,216},{28,22... | collective-permute-start | bytes 258056 | tf_op jit(solution)/shard_map/ppermute | solution.py:58
  74.8 5.8 %collective-permute-start.7 = (f16[3,1,16,896]{3,2,1,0:T(8,128)(2,1)S(1)}, f16[3,1,16,896]{3,2,1,0:T(8,128)(2,1)S(1)}, u32[]{:S(2)}, u32[]{:S(2)}) collective-permute-start(f16[3,1,16,896]{3,2,1,0:T(8,128)(2,1)S(1)} %get-tuple-element.32), channel_id=1, source_target_pairs={{0,64},{4,68},{8,72},{12,76},{16,80},{20,84},{24,88},{28,92},{32,9... | collective-permute-start | bytes 258056 | tf_op jit(solution)/shard_map/ppermute | solution.py:58
  82.0 15.7 %collective-permute-start.16 = (bf16[3,1,16,896]{3,2,1,0:T(8,128)(2,1)S(1)}, bf16[3,1,16,896]{3,2,1,0:T(8,128)(2,1)S(1)}, u32[]{:S(2)}, u32[]{:S(2)}) collective-permute-start(bf16[3,1,16,896]{3,2,1,0:T(8,128)(2,1)S(1)} %get-tuple-element.21), channel_id=1, source_target_pairs={{0,128},{4,132},{8,136},{12,140},{16,144},{20,148},{24,152},{28,15... | collective-permute-start | bytes 258056 | tf_op jit(solution)/shard_map/ppermute | solution.py:58
  85.5 12.2 %collective-permute-start.17 = (bf16[3,1,16,896]{3,2,1,0:T(8,128)(2,1)S(1)}, bf16[3,1,16,896]{3,2,1,0:T(8,128)(2,1)S(1)}, u32[]{:S(2)}, u32[]{:S(2)}) collective-permute-start(bf16[3,1,16,896]{3,2,1,0:T(8,128)(2,1)S(1)} %get-tuple-element.21), channel_id=1, source_target_pairs={{0,64},{4,68},{8,72},{12,76},{16,80},{20,84},{24,88},{28,92},{32,9... | collective-permute-start | bytes 258056 | tf_op jit(solution)/shard_map/ppermute | solution.py:58
  85.9 22.3 %collective-permute-start.18 = (bf16[3,1,16,896]{3,2,1,0:T(8,128)(2,1)S(1)}, bf16[3,1,16,896]{3,2,1,0:T(8,128)(2,1)S(1)}, u32[]{:S(2)}, u32[]{:S(2)}) collective-permute-start(bf16[3,1,16,896]{3,2,1,0:T(8,128)(2,1)S(1)} %get-tuple-element.21), channel_id=1, source_target_pairs={{0,192},{4,196},{8,200},{12,204},{16,208},{20,212},{24,216},{28,22... | collective-permute-start | bytes 258056 | tf_op jit(solution)/shard_map/ppermute | solution.py:58
  89.2 6.9 %collective-permute-start.10 = (f32[1,3,8,896]{3,2,1,0:T(8,128)S(1)}, f32[1,3,8,896]{3,2,1,0:T(8,128)S(1)}, u32[]{:S(2)}, u32[]{:S(2)}) collective-permute-start(f32[1,3,8,896]{3,2,1,0:T(8,128)S(1)} %pad_maximum_fusion.5), channel_id=1, source_target_pairs={{0,8},{4,28},{8,0},{12,20},{16,24},{20,12},{24,16},{28,4},{32,40},... | collective-permute-start | bytes 258056 | tf_op jit(solution)/shard_map/ppermute | solution.py:58
  96.1 3.7 %collective-permute-start.11 = (f32[1,3,8,896]{3,2,1,0:T(8,128)S(1)}, f32[1,3,8,896]{3,2,1,0:T(8,128)S(1)}, u32[]{:S(2)}, u32[]{:S(2)}) collective-permute-start(f32[1,3,8,896]{3,2,1,0:T(8,128)S(1)} %pad_maximum_fusion.6), channel_id=1, source_target_pairs={{0,24},{4,12},{8,16},{12,4},{16,8},{20,28},{24,0},{28,20},{32,56},... | collective-permute-start | bytes 258056 | tf_op jit(solution)/shard_map/ppermute | solution.py:58
  100.0 9.2 %collective-permute-start.12 = (f32[1,3,2,3584]{3,2,1,0:T(2,128)S(1)}, f32[1,3,2,3584]{3,2,1,0:T(2,128)S(1)}, u32[]{:S(2)}, u32[]{:S(2)}) collective-permute-start(f32[1,3,2,3584]{3,2,1,0:T(2,128)S(1)} %constant_dynamic-slice_fusion.2), channel_id=1, source_target_pairs={{0,4},{4,0},{8,12},{12,8},{16,20},{20,16},{24,28},{28,24},{32,36},... | collective-permute-start | bytes 258056 | tf_op jit(solution)/shard_map/ppermute | solution.py:58
  108.2 6.5 %collective-permute-start.19 = (bf16[3,4,16,896]{3,2,1,0:T(8,128)(2,1)S(1)}, bf16[3,4,16,896]{3,2,1,0:T(8,128)(2,1)S(1)}, u32[]{:S(2)}, u32[]{:S(2)}) collective-permute-start(bf16[3,4,16,896]{3,2,1,0:T(8,128)(2,1)S(1)} %constant_dynamic-update-slice_fusion.2), channel_id=1, source_target_pairs={{0,24},{4,12},{8,16},{12,4},{16,8},{20,28},{24,0},{28,20},{32,56},... | collective-permute-start | bytes 1032200 | tf_op jit(solution)/shard_map/ppermute | solution.py:58
  109.2 5.7 %copy-start.4 = (f32[2,3,7168]{2,0,1:T(2,128)S(1)}, f32[2,3,7168]{2,0,1:T(2,128)}, u32[]{:S(2)}) copy-start(f32[2,3,7168]{2,0,1:T(2,128)} %param.12) | copy-start | bytes 516100
  109.2 5.7 %copy-start.6 = (f32[2,3,7168]{2,0,1:T(2,128)S(1)}, f32[2,3,7168]{2,0,1:T(2,128)}, u32[]{:S(2)}) copy-start(f32[2,3,7168]{2,0,1:T(2,128)} %param.11) | copy-start | bytes 516100
  114.8 7.4 %collective-permute-start.20 = (bf16[3,4,8,1792]{3,2,1,0:T(8,128)(2,1)S(1)}, bf16[3,4,8,1792]{3,2,1,0:T(8,128)(2,1)S(1)}, u32[]{:S(2)}, u32[]{:S(2)}) collective-permute-start(bf16[3,4,8,1792]{3,2,1,0:T(8,128)(2,1)S(1)} %get-tuple-element.27), channel_id=1, source_target_pairs={{0,8},{4,28},{8,0},{12,20},{16,24},{20,12},{24,16},{28,4},{32,40},... | collective-permute-start | bytes 1032200 | tf_op jit(solution)/shard_map/ppermute | solution.py:58
  116.3 10.5 %collective-permute-start.21 = (bf16[3,4,8,1792]{3,2,1,0:T(8,128)(2,1)S(1)}, bf16[3,4,8,1792]{3,2,1,0:T(8,128)(2,1)S(1)}, u32[]{:S(2)}, u32[]{:S(2)}) collective-permute-start(bf16[3,4,8,1792]{3,2,1,0:T(8,128)(2,1)S(1)} %get-tuple-element.26), channel_id=1, source_target_pairs={{0,32},{4,228},{8,40},{12,236},{16,48},{20,244},{24,56},{28,252},{... | collective-permute-start | bytes 1032200 | tf_op jit(solution)/shard_map/ppermute | solution.py:58
  122.3 11.1 %collective-permute-start.22 = (bf16[3,4,8,3584]{3,2,1,0:T(8,128)(2,1)S(1)}, bf16[3,4,8,3584]{3,2,1,0:T(8,128)(2,1)S(1)}, u32[]{:S(2)}, u32[]{:S(2)}) collective-permute-start(bf16[3,4,8,3584]{3,2,1,0:T(8,128)(2,1)S(1)} %pad_maximum_fusion), channel_id=1, source_target_pairs={{0,32},{4,228},{8,40},{12,236},{16,48},{20,244},{24,56},{28,252},{... | collective-permute-start | bytes 2064392 | tf_op jit(solution)/shard_map/ppermute | solution.py:58
  123.0 15.1 %collective-permute-start.24 = (bf16[3,4,8,3584]{3,2,1,0:T(8,128)(2,1)S(1)}, bf16[3,4,8,3584]{3,2,1,0:T(8,128)(2,1)S(1)}, u32[]{:S(2)}, u32[]{:S(2)}) collective-permute-start(bf16[3,4,8,3584]{3,2,1,0:T(8,128)(2,1)S(1)} %pad_maximum_fusion), channel_id=1, source_target_pairs={{0,4},{4,0},{8,12},{12,8},{16,20},{20,16},{24,28},{28,24},{32,36},... | collective-permute-start | bytes 2064392 | tf_op jit(solution)/shard_map/ppermute | solution.py:58
  126.9 11.1 %collective-permute-start.23 = (bf16[3,8,8,1792]{3,2,1,0:T(8,128)(2,1)S(1)}, bf16[3,8,8,1792]{3,2,1,0:T(8,128)(2,1)S(1)}, u32[]{:S(2)}, u32[]{:S(2)}) collective-permute-start(bf16[3,8,8,1792]{3,2,1,0:T(8,128)(2,1)S(1)} %bitcast.215), channel_id=1, source_target_pairs={{0,8},{4,28},{8,0},{12,20},{16,24},{20,12},{24,16},{28,4},{32,40},... | collective-permute-start | bytes 2064392 | tf_op jit(solution)/shard_map/ppermute | solution.py:58
  127.0 11.1 %collective-permute-start.25 = (bf16[3,8,8,1792]{3,2,1,0:T(8,128)(2,1)S(1)}, bf16[3,8,8,1792]{3,2,1,0:T(8,128)(2,1)S(1)}, u32[]{:S(2)}, u32[]{:S(2)}) collective-permute-start(bf16[3,8,8,1792]{3,2,1,0:T(8,128)(2,1)S(1)} %bitcast.216), channel_id=1, source_target_pairs={{0,4},{4,0},{8,12},{12,8},{16,20},{20,16},{24,28},{28,24},{32,36},... | collective-permute-start | bytes 2064392 | tf_op jit(solution)/shard_map/ppermute | solution.py:58
  133.4 4.8 %collective-permute-start.26 = (bf16[3,4,8,3584]{3,2,1,0:T(8,128)(2,1)S(1)}, bf16[3,4,8,3584]{3,2,1,0:T(8,128)(2,1)S(1)}, u32[]{:S(2)}, u32[]{:S(2)}) collective-permute-start(bf16[3,4,8,3584]{3,2,1,0:T(8,128)(2,1)S(1)} %collective-permute-done.22), channel_id=1, source_target_pairs={{0,4},{4,0},{8,12},{12,8},{16,20},{20,16},{24,28},{28,24},{32,36},... | collective-permute-start | bytes 2064392 | tf_op jit(solution)/shard_map/ppermute | solution.py:58
  138.0 2.1 %collective-permute-start.27 = (bf16[3,8,8,1792]{3,2,1,0:T(8,128)(2,1)S(1)}, bf16[3,8,8,1792]{3,2,1,0:T(8,128)(2,1)S(1)}, u32[]{:S(2)}, u32[]{:S(2)}) collective-permute-start(bf16[3,8,8,1792]{3,2,1,0:T(8,128)(2,1)S(1)} %collective-permute-done.23), channel_id=1, source_target_pairs={{0,4},{4,0},{8,12},{12,8},{16,20},{20,16},{24,28},{28,24},{32,36},... | collective-permute-start | bytes 2064392 | tf_op jit(solution)/shard_map/ppermute | solution.py:58
  140.2 2.4 %copy-start = (bf16[3,4,2,2,8,7168]{5,4,3,2,1,0:T(8,128)(2,1)}, bf16[3,4,2,2,8,7168]{5,4,3,2,1,0:T(8,128)(2,1)S(1)}, u32[]{:S(2)}) copy-start(bf16[3,4,2,2,8,7168]{5,4,3,2,1,0:T(8,128)(2,1)S(1)} %constant_dynamic-update-slice_fusion.6) | copy-start | bytes 16515076
